TPU v7x, 32 devices: a whole 2x2x4 slice. The times are simulated.
32 devices in a mesh: dp: 8 (over y, x, core), mp: 4 (over z).
Axes of the slice: x: 2, y: 2, z: 4, core: 2. Of those that a mesh axis runs over, the one named last changes fastest.
Arguments:
- token_block: int32 [8192, 1], P(('dp', 'mp')), may hold values from 0 to 31; in each aligned block of 256 rows (0 to 255, 256 to 511, ...) at most 16 rows name the same one
- token_offset: int32 [8192], P(('dp', 'mp')), may hold values from 0 to 15663
- lengths: int32 [128], P(('dp', 'mp')), may hold values from 1 to 64, as said below
- group_counts: int32 [109], replicated, may hold values from 1 to 16, 128 in all
- table: bfloat16 [501248, 768], P(('dp', 'mp')), may hold values from -6 to 6
- weight_qkv: bfloat16 [768, 2304], P(None, 'mp'), may hold values from -0.21875 to 0.21875
- bias_query: bfloat16 [768], P('mp'), may hold values from -2 to 2
- bias_value: bfloat16 [768], P('mp'), may hold values from -2 to 2
- weight_out: bfloat16 [768, 768], P('mp'), may hold values from -0.875 to 0.875
- bias_out: bfloat16 [768], replicated, may hold values from -2 to 2
- gain_one: bfloat16 [768], replicated, may hold values from 0.5 to 1.5
- shift_one: bfloat16 [768], replicated, may hold values from -2 to 2
- weight_in: bfloat16 [768, 3072], P(None, 'mp'), may hold values from -0.21875 to 0.21875
- bias_in: bfloat16 [3072], P('mp'), may hold values from -2 to 2
- weight_down: bfloat16 [3072, 768], P('mp'), may hold values from -0.15625 to 0.15625
- bias_down: bfloat16 [768], replicated, may hold values from -2 to 2
- gain_two: bfloat16 [768], replicated, may hold values from 0.5 to 1.5
- shift_two: bfloat16 [768], replicated, may hold values from -2 to 2
- cotangent: bfloat16 [8192, 768], P(('dp', 'mp')), may hold values from -6 to 6
Outputs:
- activations: bfloat16 [8192, 768], P(('dp', 'mp'))
- grad_table: float32 [501248, 768], P(('dp', 'mp'))
- grad_weight_qkv: float32 [768, 2304], P(None, 'mp')
- grad_bias_query: float32 [768], P('mp')
- grad_bias_value: float32 [768], P('mp')
- grad_weight_out: float32 [768, 768], P('mp')
- grad_bias_out: float32 [768], replicated
- grad_gain_one: float32 [768], replicated
- grad_shift_one: float32 [768], replicated
- grad_weight_in: float32 [768, 3072], P(None, 'mp')
- grad_bias_in: float32 [3072], P('mp')
- grad_weight_down: float32 [3072, 768], P('mp')
- grad_bias_down: float32 [768], replicated
- grad_gain_two: float32 [768], replicated
- grad_shift_two: float32 [768], replicated
Inputs may be any that keep to these rules, and one draw needn't show every extreme that they name: `token_block`: among the rows of one device, at most 16 tokens name the same block. `lengths`: positions from a sentence's length on are padding. `group_counts`: the counts sum to 128.
All inputs are finite; a program needn't handle non-finite values.
Results may differ from a plain program's by a relative error of at most 0.02.
Values may be sent and summed in bfloat16 or wider, within the bound.
A program may use at most 192 MiB of HBM per device.

v0:
```python
from functools import partial

import jax
import jax.numpy as jnp
from jax import lax
from jax.sharding import PartitionSpec as P

HD = 64
SEQ = 64


eps_norm = 1e-12


def norm_rows(hidden, gain_vec, shift_vec):
    row_mean = jnp.mean(hidden, axis=-1, keepdims=True)
    centred = hidden - row_mean
    variance = jnp.mean(centred * centred, axis=-1, keepdims=True)
    row_scale = lax.rsqrt(variance + eps_norm)
    normed = centred * row_scale
    return (normed * gain_vec + shift_vec, normed, row_scale)


def norm_back(grad_out, normed, row_scale, gain_vec):
    grad_normed = grad_out * gain_vec
    inner_mean = jnp.mean(grad_normed, axis=-1, keepdims=True)
    cross_mean = jnp.mean(grad_normed * normed, axis=-1, keepdims=True)
    grad_in = row_scale * (grad_normed - inner_mean - normed * cross_mean)
    return (grad_in, jnp.sum(grad_out * normed, axis=0), jnp.sum(grad_out, axis=0))


def on_device(
    token_block,
    token_offset,
    lengths,
    group_counts,
    table,
    weight_qkv,
    bias_query,
    bias_value,
    weight_out,
    bias_out,
    gain_one,
    shift_one,
    weight_in,
    bias_in,
    weight_down,
    bias_down,
    gain_two,
    shift_two,
    cotangent,
):
    f32 = jnp.float32
    bf16 = jnp.bfloat16
    devices = lax.axis_size(("dp", "mp"))
    tok_rows = token_offset.shape[0]
    model_width = table.shape[1]
    capacity = max(2, 2 * tok_rows // devices)
    token_owner = token_block[:, 0]
    owner_hits = (token_owner[:, None] == jnp.arange(devices, dtype=jnp.int32)[None, :]).astype(
        jnp.int32
    )
    slot_index = jnp.sum((jnp.cumsum(owner_hits, axis=0) - 1) * owner_hits, axis=1)
    slot_place = token_owner * capacity + slot_index
    requests = jnp.full((devices * capacity,), -1, jnp.int32).at[slot_place].set(token_offset)
    wanted = lax.all_to_all(
        requests.reshape(devices, capacity), ("dp", "mp"), split_axis=0, concat_axis=0, tiled=True
    )
    slot_live = wanted >= 0
    wanted_rows = jnp.maximum(wanted, 0)
    fetched = lax.all_to_all(
        table[wanted_rows], ("dp", "mp"), split_axis=0, concat_axis=0, tiled=True
    )
    embedded = fetched.reshape(devices * capacity, model_width)[slot_place]
    sent_local = lengths.shape[0]
    total_sent = sent_local * devices
    group_num = group_counts.shape[0]
    sent_index = lax.axis_index(("dp", "mp")) * sent_local + jnp.arange(sent_local, dtype=jnp.int32)
    offsets = jnp.cumsum(group_counts) - group_counts
    member = (sent_index[:, None] >= offsets[None, :]) & (
        sent_index[:, None] < (offsets + group_counts)[None, :]
    )
    group_weight = total_sent / (group_num * group_counts.astype(f32))
    sent_weight = jnp.sum(jnp.where(member, group_weight[None, :], f32(0.0)), axis=1)
    positions = jnp.arange(SEQ, dtype=f32)
    token_live = (positions[None, :] < lengths[:, None].astype(f32)).astype(f32)
    row_weight = (token_live * sent_weight[:, None]).reshape(tok_rows)
    count_local = jnp.sum(lengths).astype(f32)
    whole_in, whole_len = (
        lax.all_gather(embedded, "mp", axis=0, tiled=True),
        lax.all_gather(lengths.astype(bf16), "mp", axis=0, tiled=True),
    )
    rows_all = whole_in.shape[0]
    sentences_all = whole_len.shape[0]
    head_count = weight_qkv.shape[1] // (3 * HD)
    block_sent = min(8, sentences_all)
    block_count = sentences_all // block_sent
    mixed_qkv = jnp.dot(whole_in, weight_qkv, preferred_element_type=f32).reshape(
        rows_all, head_count, 3, HD
    )
    block_shape = (block_count, block_sent, SEQ, head_count, HD)
    queries = (
        (mixed_qkv[:, :, 0, :] + bias_query.astype(f32).reshape(head_count, HD))
        .astype(bf16)
        .reshape(block_shape)
    )
    key_rows = mixed_qkv[:, :, 1, :].astype(bf16).reshape(block_shape)
    value_rows = (
        (mixed_qkv[:, :, 2, :] + bias_value.astype(f32).reshape(head_count, HD))
        .astype(bf16)
        .reshape(block_shape)
    )
    len_blocks = whole_len.astype(f32).reshape(block_count, block_sent)

    def block_scores(q_blk, k_blk, len_blk):
        scores = jnp.einsum("sqhe,skhe->shqk", q_blk, k_blk, preferred_element_type=f32) * 0.125
        key_valid = positions[None, :] < len_blk[:, None]
        return jnp.where(key_valid[:, None, None, :], scores, f32(-1e30))

    def attend(block_items):
        q_blk, k_blk, v_blk, len_blk = block_items
        scores = block_scores(q_blk, k_blk, len_blk)
        row_max = jnp.max(scores, axis=-1, keepdims=True)
        exp_total = jnp.sum(jnp.exp(scores - row_max), axis=-1, keepdims=True)
        log_total = row_max + jnp.log(exp_total)
        attn_probs = jnp.exp(scores - log_total)
        context_blk = jnp.einsum(
            "shqk,skhe->sqhe", attn_probs.astype(bf16), v_blk, preferred_element_type=f32
        ).astype(bf16)
        return (context_blk, log_total[..., 0])

    context_blocks, log_totals = lax.map(attend, (queries, key_rows, value_rows, len_blocks))
    context = context_blocks.reshape(rows_all, head_count * HD)
    attn_sum = lax.psum_scatter(
        jnp.dot(context, weight_out, preferred_element_type=f32),
        "mp",
        scatter_dimension=0,
        tiled=True,
    )
    gain_one_f = gain_one.astype(f32)
    gain_two_f = gain_two.astype(f32)
    first_out, normed_one, scale_one = norm_rows(
        embedded.astype(f32) + attn_sum + bias_out.astype(f32), gain_one_f, shift_one.astype(f32)
    )
    whole_first = lax.all_gather(first_out.astype(bf16), "mp", axis=0, tiled=True)
    hidden_pre = jnp.dot(whole_first, weight_in, preferred_element_type=f32) + bias_in.astype(f32)
    gelu_val, gelu_pull = jax.vjp(partial(jax.nn.gelu, approximate=False), hidden_pre)
    hidden_act = gelu_val.astype(bf16)
    down_sum = lax.psum_scatter(
        jnp.dot(
            lax.slice_in_dim(hidden_act, 0, tok_rows * lax.axis_size("mp"), axis=0),
            weight_down,
            preferred_element_type=f32,
        ),
        "mp",
        scatter_dimension=0,
        tiled=True,
    )
    final_out, normed_two, scale_two = norm_rows(
        first_out + down_sum + bias_down.astype(f32), gain_two_f, shift_two.astype(f32)
    )
    activations = final_out.astype(bf16)
    grad_final = row_weight[:, None] * cotangent.astype(f32)
    grad_h2, grad_gain_two, grad_shift_two = norm_back(
        grad_final, normed_two, scale_two, gain_two_f
    )
    grad_bias_down = jnp.sum(grad_h2, axis=0)
    whole_grad_down = lax.all_gather(grad_h2.astype(bf16), "mp", axis=0, tiled=True)
    grad_weight_down = jnp.einsum(
        "rf,rd->fd", hidden_act, whole_grad_down, preferred_element_type=f32
    )
    grad_act = jnp.einsum("rd,fd->rf", whole_grad_down, weight_down, preferred_element_type=f32)
    grad_pre = gelu_pull(grad_act)[0].astype(bf16)
    grad_bias_in = jnp.sum(grad_pre.astype(f32), axis=0)
    grad_weight_in = jnp.einsum("rd,rf->df", whole_first, grad_pre, preferred_element_type=f32)
    grad_first = grad_h2 + lax.psum_scatter(
        jnp.einsum("rf,df->rd", grad_pre, weight_in, preferred_element_type=f32),
        "mp",
        scatter_dimension=0,
        tiled=True,
    )
    grad_h1, grad_gain_one, grad_shift_one = norm_back(
        grad_first, normed_one, scale_one, gain_one_f
    )
    grad_bias_out = jnp.sum(grad_h1, axis=0)
    whole_grad_attn = lax.all_gather(grad_h1.astype(bf16), "mp", axis=0, tiled=True)
    grad_weight_out = jnp.einsum("rc,rd->cd", context, whole_grad_attn, preferred_element_type=f32)
    grad_context = (
        jnp.einsum("rd,cd->rc", whole_grad_attn, weight_out, preferred_element_type=f32)
        .astype(bf16)
        .reshape(block_shape)
    )

    def attend_back(block_items):
        q_blk, k_blk, v_blk, len_blk, log_blk, dctx_blk = block_items
        scores = block_scores(q_blk, k_blk, len_blk)
        attn_probs = jnp.exp(scores - log_blk[..., None])
        grad_probs = jnp.einsum("sqhe,skhe->shqk", dctx_blk, v_blk, preferred_element_type=f32)
        grad_value = jnp.einsum(
            "shqk,sqhe->skhe", attn_probs.astype(bf16), dctx_blk, preferred_element_type=f32
        ).astype(bf16)
        grad_scores = (
            attn_probs * (grad_probs - jnp.sum(grad_probs * attn_probs, axis=-1, keepdims=True))
        ).astype(bf16)
        grad_query = (
            jnp.einsum("shqk,skhe->sqhe", grad_scores, k_blk, preferred_element_type=f32) * 0.125
        ).astype(bf16)
        grad_key = (
            jnp.einsum("shqk,sqhe->skhe", grad_scores, q_blk, preferred_element_type=f32) * 0.125
        ).astype(bf16)
        return jnp.stack([grad_query, grad_key, grad_value], axis=3)

    grad_mixed = lax.map(
        attend_back, (queries, key_rows, value_rows, len_blocks, log_totals, grad_context)
    )
    grad_mixed = grad_mixed.reshape(rows_all, head_count * 3 * HD)
    grad_weight_qkv = jnp.einsum("rd,rc->dc", whole_in, grad_mixed, preferred_element_type=f32)
    grad_parts = jnp.sum(grad_mixed.astype(f32).reshape(rows_all, head_count, 3, HD), axis=0)
    grad_bias_query = grad_parts[:, 0, :].reshape(head_count * HD)
    grad_bias_value = grad_parts[:, 2, :].reshape(head_count * HD)
    grad_embed = grad_h1 + lax.psum_scatter(
        jnp.einsum("rc,dc->rd", grad_mixed, weight_qkv, preferred_element_type=f32).astype(
            jnp.bfloat16
        ),
        "mp",
        scatter_dimension=0,
        tiled=True,
    ).astype(jnp.float32)
    (
        count_all,
        sum_gain_one,
        sum_shift_one,
        sum_bias_out,
        sum_gain_two,
        sum_shift_two,
        sum_bias_down,
    ) = lax.psum(
        (
            count_local,
            grad_gain_one,
            grad_shift_one,
            grad_bias_out,
            grad_gain_two,
            grad_shift_two,
            grad_bias_down,
        ),
        ("dp", "mp"),
    )
    factor = lax.rsqrt(count_all)
    sum_qkv, sum_query, sum_value, sum_out, sum_in, sum_bias_in, sum_down = (
        lax.psum(grad_weight_qkv.astype(jnp.bfloat16), "dp").astype(jnp.float32),
        lax.psum(grad_bias_query.astype(jnp.bfloat16), "dp").astype(jnp.float32),
        lax.psum(grad_bias_value.astype(jnp.bfloat16), "dp").astype(jnp.float32),
        lax.psum(grad_weight_out.astype(jnp.bfloat16), "dp").astype(jnp.float32),
        lax.psum(grad_weight_in.astype(jnp.bfloat16), "dp").astype(jnp.float32),
        lax.psum(grad_bias_in.astype(jnp.bfloat16), "dp").astype(jnp.float32),
        lax.psum(grad_weight_down.astype(jnp.bfloat16), "dp").astype(jnp.float32),
    )
    outgoing = (
        jnp.zeros((devices * capacity, model_width), f32)
        .at[slot_place]
        .set(grad_embed)
        .reshape(devices, capacity, model_width)
    )
    incoming = lax.all_to_all(
        outgoing.astype(jnp.bfloat16), ("dp", "mp"), split_axis=0, concat_axis=0, tiled=True
    ).astype(outgoing.dtype)
    received = jnp.where(slot_live[..., None], incoming, f32(0.0)).reshape(
        devices * capacity, model_width
    )
    grad_table = jnp.zeros(table.shape, f32).at[wanted_rows.reshape(-1)].add(received) * factor
    return (
        activations,
        grad_table,
        sum_qkv * factor,
        sum_query * factor,
        sum_value * factor,
        sum_out * factor,
        sum_bias_out * factor,
        sum_gain_one * factor,
        sum_shift_one * factor,
        sum_in * factor,
        sum_bias_in * factor,
        sum_down * factor,
        sum_bias_down * factor,
        sum_gain_two * factor,
        sum_shift_two * factor,
    )


def solution(mesh):
    placed = (
        P(("dp", "mp"), None),
        P(("dp", "mp")),
        P(("dp", "mp")),
        P(),
        P(("dp", "mp"), None),
        P(None, "mp"),
        P("mp"),
        P("mp"),
        P("mp", None),
        P(),
        P(),
        P(),
        P(None, "mp"),
        P("mp"),
        P("mp", None),
        P(),
        P(),
        P(),
        P(("dp", "mp"), None),
    )
    return jax.shard_map(
        on_device,
        mesh=mesh,
        in_specs=placed,
        out_specs=(
            P(("dp", "mp"), None),
            P(("dp", "mp"), None),
            P(None, "mp"),
            P("mp"),
            P("mp"),
            P("mp", None),
            P(),
            P(),
            P(),
            P(None, "mp"),
            P("mp"),
            P("mp", None),
            P(),
            P(),
            P(),
        ),
        check_vma=False,
    )
```

profile of v0, /device:TPU:1, one launch (start us, length us, event | category | flops | bytes accessed | tf_op | source)
XLA Modules:
  0.0 689.3 jit_solution(15730359723597608846)
XLA Ops:
  11.9 13.6 %all_to_all.19 = s32[32,1,16]{2,1,0:T(1,128)S(1)} all-to-all(s32[32,1,16]{2,1,0:T(1,128)S(1)} %bitcast.198), channel_id=1, replica_groups=mesh['dp'=8,'mp'=4] {'dp','mp'}, dimensions={0} | all-to-all | bytes 4096 | tf_op jit(solution)/shard_map/all_to_all | solution.py:66
  25.7 14.0 %gather_fusion = bf16[512,768]{1,0:T(8,128)(2,1)} fusion(bf16[15664,768]{1,0:T(8,128)(2,1)} %param.27, s32[1024]{0:T(1024)S(1)} %pad_clamp_fusion.1), kind=kCustom, calls=%fused_computation | custom fusion | bytes 1574912 | tf_op jit(solution)/shard_map/gather | solution.py:72
  43.0 20.9 %all-to-all-done.1 = bf16[32,16,768]{2,1,0:T(8,128)(2,1)S(1)} async-done(((bf16[32,16,768]{2,1,0:T(8,128)(2,1)}), bf16[32,16,768]{2,1,0:T(8,128)(2,1)S(1)}, u32[]{:S(2)}, u32[]{:S(2)}) %all-to-all-start.1) | async-done | bytes 786464 | tf_op jit(solution)/shard_map/all_to_all | solution.py:71
  68.5 7.9 %all-reduce = bf16[16]{0:T(256)(128)(2,1)S(1)} all-reduce(bf16[16]{0:T(256)(128)(2,1)S(1)} %dynamic-update-slice), channel_id=1, replica_groups=mesh['dp'=8,'mp'=4] {'mp'}, use_global_device_ids=true, to_apply=%add | all-reduce | flops 16 | bytes 64
  77.2 23.5 %all-gather.12.cloned.1.call-done = bf16[1024,768]{1,0:T(8,128)(2,1)} async-done(((bf16[256,768]{1,0:T(8,128)(2,1)}), bf16[1024,768]{1,0:T(8,128)(2,1)}) %all-gather.12.cloned.1.call-update) | async-done | bytes 1572880 | tf_op jit(solution)/shard_map/all_gather | solution.py:90
  114.3 4.8 while.24
  127.2 57.4 %reduce-scatter.5.cloned.1.call-done = f32[256,768]{1,0:T(8,128)} async-done(((f32[1024,768]{1,0:T(8,128)}), f32[256,768]{1,0:T(8,128)}) %reduce-scatter.5.cloned.1.call-update) | async-done | bytes 786448 | tf_op jit(solution)/shard_map/reduce_scatter | solution.py:134
  189.9 35.1 %all-gather.6.cloned.1.call-done = bf16[1024,768]{1,0:T(8,128)(2,1)} async-done(((bf16[256,768]{1,0:T(8,128)(2,1)}), bf16[1024,768]{1,0:T(8,128)(2,1)}) %all-gather.6.cloned.1.call-update) | async-done | bytes 1572880 | tf_op jit(solution)/shard_map/all_gather | solution.py:145
  225.1 10.6 %multiply_convert_fusion.1 = (bf16[1024,768]{1,0:T(8,128)(2,1)S(1)}, f32[1024,768]{1,0:T(8,128)}, f32[1024,768]{1,0:T(8,128)}) fusion(f32[768]{0:T(1024)} %convert_element_type.189, bf16[1024,768]{1,0:T(8,128)(2,1)} %all-gather.6.cloned.1.call-done, bf16[768,768]{1,0:T(8,128)(2,1)S(1)} %copy-done), kind=kOutput, calls=%fused_computation.71 | convolution fusion | flops 1259864064 | bytes 10619904 | tf_op jit(solution)/shard_map/dot_general | solution.py:146
  253.1 46.8 %reduce-scatter.7.cloned.1.call-done = f32[256,768]{1,0:T(8,128)} async-done(((f32[1024,768]{1,0:T(8,128)}), f32[256,768]{1,0:T(8,128)}) %reduce-scatter.7.cloned.1.call-update) | async-done | bytes 786448 | tf_op jit(solution)/shard_map/reduce_scatter | solution.py:149
  306.1 36.5 %all-gather.8.cloned.1.call-done = bf16[1024,768]{1,0:T(8,128)(2,1)} async-done(((bf16[256,768]{1,0:T(8,128)(2,1)}), bf16[1024,768]{1,0:T(8,128)(2,1)}) %all-gather.8.cloned.1.call-update) | async-done | bytes 1572880 | tf_op jit(solution)/shard_map/all_gather | solution.py:168
  342.7 6.4 fusion.61
  353.4 59.9 %reduce-scatter.9.cloned.1.call-done = f32[256,768]{1,0:T(8,128)} async-done(((f32[1024,768]{1,0:T(8,128)}), f32[256,768]{1,0:T(8,128)}) %reduce-scatter.9.cloned.1.call-update) | async-done | bytes 786448 | tf_op jit(solution)/shard_map/reduce_scatter | solution.py:176
  417.5 36.3 %all-gather.10.cloned.1.call-done = bf16[1024,768]{1,0:T(8,128)(2,1)} async-done(((bf16[256,768]{1,0:T(8,128)(2,1)}), bf16[1024,768]{1,0:T(8,128)(2,1)}) %all-gather.10.cloned.1.call-update) | async-done | bytes 1572880 | tf_op jit(solution)/shard_map/all_gather | solution.py:186
  456.5 16.8 %while.25 = (s32[]{:T(128)}, bf16[2,8,64,3,3,64]{5,2,3,1,4,0:T(8,128)(2,1)}, bf16[2,8,64,3,64]{4,2,3,1,0:T(8,128)(2,1)S(1)}, f32[2,8]{1,0:T(2,128)S(1)}, bf16[2,...) while((s32[]{:T(128)}, ...), condition=%wide.region_23.24_spmd.clone, body=%wide.region_21.23_spmd.clone.sunk | while | flops 66059264 | bytes 22653772 | solution.py:213
  479.4 4.2 convolution_convert_fusion.2
  484.4 4.0 convolution_convert_fusion.3
  491.1 41.5 %all-reduce.1 = (f32[]{:T(128)}, f32[768]{0:T(1024)S(1)}, f32[768]{0:T(1024)S(1)}, f32[768]{0:T(1024)S(1)}, f32[768]{0:T(1024)S(1)}, /*index=5*/f32[768]{0:T(1024)S(1)}, f32[768]{0:T(1024)S(1)}) all-reduce(f32[]{:T(128)S(6)} %convert_element_type.207, f32[768]{0:T(1024)S(1)} %copy-done.29, ...), channel_id=1, replica_groups=mesh['dp'=8,'mp'=4] {'dp','mp'}, use_global_device_ids=true, to_apply=%region_28.29 | all-reduce | flops 4609 | bytes 36872 | tf_op jit(solution)/shard_map/psum | solution.py:237
  535.6 3.8 convolution_convert_fusion.5
  542.6 13.3 %all-reduce.2 = (bf16[192]{0:T(256)(128)(2,1)S(1)}, bf16[192]{0:T(256)(128)(2,1)S(1)}, bf16[768]{0:T(1024)(128)(2,1)S(1)}) all-reduce(bf16[192]{0:T(256)(128)(2,1)S(1)} %convert_element_type.211, bf16[192]{0:T(256)(128)(2,1)S(1)} %convert_element_type.213, bf16[768]{0:T(1024)(128)(2,1)S(1)} %copy-done.35), channel_id=1, replica_groups=mesh['dp'=8,'mp'=4] {'dp'}, use_global_device_ids=true, to_apply=%region_31.32 | all-reduce | flops 1152 | bytes 4608 | tf_op jit(solution)/shard_map/psum | solution.py:252
  559.8 4.7 all-to-all-start.2
  565.7 51.8 %all-reduce.6.cloned.1.call-done = (bf16[768,576]{0,1:T(8,128)(2,1)}, bf16[192,768]{1,0:T(8,128)(2,1)}, bf16[768,768]{1,0:T(8,128)(2,1)}, bf16[768,768]{1,0:T(8,128)(2,1)}) async-done(((bf16[768,576]{0,1:T(8,128)(2,1)}, bf16[192,768]{1,0:T(8,128)(2,1)}, bf16[768,768]{1,0:T(8,128)(2,1)}, bf16[768,768]{1,0:T(8,128)(2,1)}), (bf16[768,576]{0,1:T(8,128)(2,1)}, bf16[192,768]{1,0:T(8,128)(2,1)}, ...) | async-done | bytes 3538960 | tf_op jit(solution)/shard_map/psum | solution.py:251
  625.4 23.8 %scatter_custom_fusion.2 = f32[15664,768]{1,0:T(8,128)} fusion(s32[512]{0:T(512)} %copy-done.32, f32[512,768]{1,0:T(8,128)S(1)} %bitcast.197, f32[]{:T(128)} %constant.48.clone.1), kind=kCustom, calls=%fused_computation.66 | custom fusion | flops 393216 | bytes 48120320 | tf_op jit(solution)/shard_map/scatter-add | solution.py:271
  649.2 33.1 %broadcast_multiply_fusion = f32[15664,768]{1,0:T(8,128)} fusion(f32[15664,768]{1,0:T(8,128)} %scatter_custom_fusion.2, f32[]{:T(128)S(6)} %rsqrt.21), kind=kLoop, calls=%fused_computation.65 | loop fusion | flops 12029952 | bytes 96239616 | tf_op jit(solution)/shard_map/mul | solution.py:271
  (278 shorter events, 123.0 us)
Async XLA Ops:
  7.2 217.9 %copy-start = (bf16[768,768]{1,0:T(8,128)(2,1)S(1)}, bf16[768,768]{1,0:T(8,128)(2,1)}, u32[]{:S(2)}) copy-start(bf16[768,768]{1,0:T(8,128)(2,1)} %param.35) | copy-start | bytes 3538948
  10.2 32.7 %copy-start.33 = (s32[256,1]{0,1:T(1,128)}, s32[256,1]{0,1:T(1,128)S(1)}, u32[]{:S(2)}) copy-start(s32[256,1]{0,1:T(1,128)S(1)} %compare_select_fusion) | copy-start | bytes 3076
  39.8 26.1 %copy-start.44 = (u32[32]{0:T(128)S(1)}, u32[32]{0:T(128)}, u32[]{:S(2)}) copy-start(u32[32]{0:T(128)} %constant.171) | copy-start | bytes 388
  39.8 27.4 %copy-start.38 = (s32[4]{0:T(128)S(1)}, s32[4]{0:T(128)}, u32[]{:S(2)}) copy-start(s32[4]{0:T(128)} %param.25) | copy-start | bytes 52
  39.8 37.2 %copy-start.36 = (bf16[192]{0:T(256)(128)(2,1)S(1)}, bf16[192]{0:T(256)(128)(2,1)}, u32[]{:S(2)}) copy-start(bf16[192]{0:T(256)(128)(2,1)} %param.29) | copy-start | bytes 1156
  39.8 37.3 %copy-start.37 = (bf16[192]{0:T(256)(128)(2,1)S(1)}, bf16[192]{0:T(256)(128)(2,1)}, u32[]{:S(2)}) copy-start(bf16[192]{0:T(256)(128)(2,1)} %param.30) | copy-start | bytes 1156
  39.8 24.1 %all-to-all-start.1 = ((bf16[32,16,768]{2,1,0:T(8,128)(2,1)}), bf16[32,16,768]{2,1,0:T(8,128)(2,1)S(1)}, u32[]{:S(2)}, u32[]{:S(2)}) async-start(bf16[32,16,768]{2,1,0:T(8,128)(2,1)} %bitcast.6), calls=%async_computation.1 | async-start | bytes 1572864 | tf_op jit(solution)/shard_map/all_to_all | solution.py:71
  42.9 57.8 %all-gather.12.cloned.1.call-start = ((), (), s32[]{:S(2)}) async-start(), calls=%async_computation.14 | async-start | bytes 1966080 | tf_op jit(solution)/shard_map/all_gather | solution.py:90
  65.8 118.8 %reduce-scatter.5.cloned.1.call-start = ((), (), s32[]{:S(2)}) async-start(), calls=%async_computation.7 | async-start | bytes 3932160 | tf_op jit(solution)/shard_map/reduce_scatter | solution.py:134
  125.1 99.9 %all-gather.6.cloned.1.call-start = ((), (), s32[]{:S(2)}) async-start(), calls=%async_computation.8 | async-start | bytes 1966080 | tf_op jit(solution)/shard_map/all_gather | solution.py:145
  188.4 111.4 %reduce-scatter.7.cloned.1.call-start = ((), (), s32[]{:S(2)}) async-start(), calls=%async_computation.9 | async-start | bytes 3932160 | tf_op jit(solution)/shard_map/reduce_scatter | solution.py:149
  240.0 102.7 %all-gather.8.cloned.1.call-start = ((), (), s32[]{:S(2)}) async-start(), calls=%async_computation.10 | async-start | bytes 1966080 | tf_op jit(solution)/shard_map/all_gather | solution.py:168
  306.1 107.2 %reduce-scatter.9.cloned.1.call-start = ((), (), s32[]{:S(2)}) async-start(), calls=%async_computation.11 | async-start | bytes 3932160 | tf_op jit(solution)/shard_map/reduce_scatter | solution.py:176
  353.4 59.9 %copy-start.11 = (f32[256,768]{1,0:T(8,128)S(1)}, f32[256,768]{1,0:T(8,128)}, u32[]{:S(2)}) copy-start(f32[256,768]{1,0:T(8,128)} %copy-done.10) | copy-start | bytes 2359300
  353.4 59.9 %copy-start.23 = (f32[256]{0:T(256)S(1)}, f32[256]{0:T(256)}, u32[]{:S(2)}) copy-start(f32[256]{0:T(256)} %copy-done.22) | copy-start | bytes 3076
  353.4 100.5 %all-gather.10.cloned.1.call-start = ((), (), s32[]{:S(2)}) async-start(), calls=%async_computation.12 | async-start | bytes 1966080 | tf_op jit(solution)/shard_map/all_gather | solution.py:186
  416.4 37.5 %copy-start.8 = (f32[256,768]{1,0:T(8,128)}, f32[256,768]{1,0:T(8,128)S(1)}, u32[]{:S(2)}) copy-start(f32[256,768]{1,0:T(8,128)S(1)} %get-tuple-element.276) | copy-start | bytes 2359300
  416.4 40.1 %copy-start.43 = (f32[2,8]{1,0:T(2,128)S(1)}, f32[2,8]{1,0:T(2,128)}, u32[]{:S(2)}) copy-start(f32[2,8]{1,0:T(2,128)} %reshape.323) | copy-start | bytes 196
  417.3 139.2 %reduce-scatter.11.cloned.1.call-start = ((), (), s32[]{:S(2)}) async-start(), calls=%async_computation.13 | async-start | bytes 1966080 | tf_op jit(solution)/shard_map/reduce_scatter | solution.py:221
  483.6 133.9 %all-reduce.6.cloned.1.call-start = ((), (), s32[]{:S(2)}) async-start(), calls=%async_computation.15 | async-start | bytes 7077888 | tf_op jit(solution)/shard_map/psum | solution.py:251
  488.5 45.9 %copy-start.12 = (bf16[1024,192]{0,1:T(8,128)(2,1)S(1)}, bf16[1024,192]{0,1:T(8,128)(2,1)}, u32[]{:S(2)}) copy-start(bf16[1024,192]{0,1:T(8,128)(2,1)} %reshape.315) | copy-start | bytes 1179652
  488.5 45.9 %copy-start.13 = (bf16[1024,768]{1,0:T(8,128)(2,1)S(1)}, bf16[1024,768]{1,0:T(8,128)(2,1)}, u32[]{:S(2)}) copy-start(bf16[1024,768]{1,0:T(8,128)(2,1)} %all-gather.10.cloned.1.call-done) | copy-start | bytes 4718596
  559.8 65.3 %all-to-all-start.2 = ((bf16[32,16,768]{2,1,0:T(8,128)(2,1)}), bf16[32,16,768]{2,1,0:T(8,128)(2,1)S(1)}, u32[]{:S(2)}, u32[]{:S(2)}) async-start(bf16[32,16,768]{2,1,0:T(8,128)(2,1)} %bitcast.12), calls=%async_computation.6 | async-start | bytes 1572864 | tf_op jit(solution)/shard_map/all_to_all | solution.py:265
  649.2 33.1 %copy-start.1 = (bf16[768,768]{1,0:T(8,128)(2,1)S(1)}, bf16[768,768]{1,0:T(8,128)(2,1)}, u32[]{:S(2)}) copy-start(bf16[768,768]{1,0:T(8,128)(2,1)} %param.35) | copy-start | bytes 3538948
  (43 other events, 135.0 us)
Sparse Core Ops, SparseCore 0:
  65.9 34.7 all-gather.11
  125.2 59.2 reduce-scatter.4
  188.6 36.4 all-gather.5
  240.1 59.7 reduce-scatter.6
  306.2 36.4 all-gather.7
  353.5 59.7 reduce-scatter.8
  417.4 36.4 all-gather.9
  483.8 35.4 reduce-scatter.10
  539.6 77.8 all-reduce.5
where the time goes:
time: 697 us; the launch traced here: 689 us
  waiting for transfers between devices  368 us (53%)
  other arithmetic  109 us (16%)
  blocking collectives  76.3 us (11%)
  local copies, waits for them, and re-layouts  58.3 us (8%)
  matrix products  51.5 us (7%)
  between operations  16.8 us (2%)
  starting transfers between devices  8.6 us (1%)
    reduce_scatter x1, waiting for transfers between devices, on_device(): lax.psum_scatter(jnp.einsum('rf,df->rd', grad_pre, weight_in, preferred_e...  59.9 us
    reduce_scatter x1, waiting for transfers between devices, on_device(): lax.psum_scatter(jnp.dot(context, weight_out, preferred_element_type=f32)...  57.4 us
    psum x1, waiting for transfers between devices, on_device(): lax.psum(grad_weight_qkv.astype(jnp.bfloat16), 'dp').astype(jnp.float32)  51.8 us
    reduce_scatter x1, waiting for transfers between devices, on_device(): lax.psum_scatter(jnp.dot(lax.slice_in_dim(hidden_act, 0, tok_rows * lax.a...  46.8 us
    psum x1, blocking collectives, on_device(): lax.psum((count_local, grad_gain_one, grad_shift_one, grad_bias_out, grad...  41.5 us
    all_gather x1, waiting for transfers between devices, on_device(): lax.all_gather(grad_h2.astype(bf16), 'mp', axis=0, tiled=True)  36.5 us
    all_gather x1, waiting for transfers between devices, on_device(): lax.all_gather(grad_h1.astype(bf16), 'mp', axis=0, tiled=True)  36.3 us
    all_gather x1, waiting for transfers between devices, on_device(): lax.all_gather(first_out.astype(bf16), 'mp', axis=0, tiled=True)  35.1 us
  transfers between devices with their start and end apart: 11, of which 9 were waited for; matrix products, arithmetic and copies ran while one was open for 7% of the time, Pallas kernels for 0%

commit v1 on v0

v1 whole, which is shorter than its diff:
```python
from functools import partial

import jax
import jax.numpy as jnp
from jax import lax
from jax.experimental import pallas as pl
from jax.experimental.pallas import tpu as pltpu
from jax.sharding import PartitionSpec as P

HD = 64
SEQ = 64
EPS = 1e-12
MESH = pl.DeviceIdType.MESH
F32 = jnp.float32
BF16 = jnp.bfloat16

INNER = 8
BLOCKS = 3


def position():
    d = lax.axis_index("dp")
    m = lax.axis_index("mp")
    core = lax.rem(d, 2)
    first = 4 - 2 * core
    second = 2 + 2 * core
    return d, m, first, second


def flip(d, bit):
    return d + bit - 2 * bit * lax.rem(lax.div(d, bit), 2)


def enter(d, m, mp):
    barrier = pltpu.get_barrier_semaphore()
    peers = [(flip(d, bit), m) for bit in (1, 2, 4)] + [(d, lax.rem(m + k, mp)) for k in range(1, mp)]
    for peer in peers:
        pl.semaphore_signal(barrier, inc=1, device_id=peer, device_id_type=MESH)
    pl.semaphore_wait(barrier, len(peers))


def remote(src, dst, send, recv, peer):
    return pltpu.make_async_remote_copy(
        src_ref=src, dst_ref=dst, send_sem=send, recv_sem=recv, device_id=peer, device_id_type=MESH
    )


def gather_kernel(mp, own_ref, out_ref, send, recv, own_sem):
    d, m, first, second = position()
    enter(d, m, mp)
    s = lax.rem(d, INNER)
    s1 = flip(s, first)
    s2 = flip(s, second)
    s3 = flip(s1, second)
    for a in range(BLOCKS):
        pltpu.make_async_copy(own_ref.at[a], out_ref.at[a, m], own_sem.at[a]).start()
    z_copies = []
    for a in range(BLOCKS):
        for k in range(1, mp):
            copy = remote(
                own_ref.at[a, s], out_ref.at[a, m, s], send.at[a, k, 0], recv.at[a, mp - k, 0], (d, lax.rem(m + k, mp))
            )
            copy.start()
            z_copies.append(copy)

    def hop(a, k, piece, slot, bit):
        ref = out_ref.at[a, lax.rem(m + k, mp), piece]
        return remote(ref, ref, send.at[a, k, slot], recv.at[a, k, slot], (flip(d, bit), m))

    units = [(a, k) for a in range(BLOCKS) for k in range(1, mp)]
    sent = []

    def go(copy):
        copy.start()
        sent.append(copy)

    def wait_z(a, k):
        ref = out_ref.at[a, lax.rem(m + k, mp), s]
        remote(ref, ref, send.at[a, k, 0], recv.at[a, k, 0], (d, lax.rem(m + k, mp))).wait_recv()

    for t in range(len(units) + 3):
        if t < len(units):
            a, k = units[t]
            wait_z(a, k)
            go(hop(a, k, s, 1, first))
            go(hop(a, k, s, 2, second))
            go(hop(a, k, s, 4, 1))
        if 0 <= t - 1 < len(units):
            a, k = units[t - 1]
            hop(a, k, s1, 1, first).wait_recv()
            go(hop(a, k, s1, 3, second))
            go(hop(a, k, s1, 5, 1))
        if 0 <= t - 2 < len(units):
            a, k = units[t - 2]
            hop(a, k, s2, 2, second).wait_recv()
            go(hop(a, k, s2, 6, 1))
            hop(a, k, s3, 3, second).wait_recv()
            go(hop(a, k, s3, 7, 1))
        if 0 <= t - 3 < len(units):
            a, k = units[t - 3]
            for slot, piece in ((4, s), (5, s1), (6, s2), (7, s3)):
                hop(a, k, flip(piece, 1), slot, 1).wait_recv()
    for copy in z_copies + sent:
        copy.wait_send()
    for a in range(BLOCKS):
        pltpu.make_async_copy(own_ref.at[a], out_ref.at[a, m], own_sem.at[a]).wait()


def gather_weights(own, mp):
    _, inner, rows, width = own.shape
    return pl.pallas_call(
        partial(gather_kernel, mp),
        out_shape=jax.ShapeDtypeStruct((BLOCKS, mp, inner, rows, width), BF16),
        in_specs=[pl.BlockSpec(memory_space=pltpu.VMEM)],
        out_specs=pl.BlockSpec(memory_space=pltpu.VMEM),
        scratch_shapes=[
            pltpu.SemaphoreType.DMA((BLOCKS, mp, 8)),
            pltpu.SemaphoreType.DMA((BLOCKS, mp, 8)),
            pltpu.SemaphoreType.DMA((BLOCKS,)),
        ],
        compiler_params=pltpu.CompilerParams(
            collective_id=0, has_side_effects=True, vmem_limit_bytes=60 * 1024 * 1024
        ),
    )(own)


def reduce_kernel(mp, grad_ref, out_ref, near, mid, far, line, send, recv):
    d, m, first, second = position()
    enter(d, m, mp)
    s = lax.rem(d, INNER)
    s1 = flip(s, first)
    s2 = flip(s, second)
    s3 = flip(s1, second)
    mine = (s, s1, s2, s3)
    other = tuple(flip(piece, 1) for piece in (s, s2, s1, s3))
    sent = []

    def go(copy):
        copy.start()
        sent.append(copy)

    units = [(a, k) for a in range(BLOCKS) for k in (*range(1, mp), 0)]

    def add(into, more):
        into[...] = (into[...].astype(F32) + more[...].astype(F32)).astype(BF16)

    def near_copy(a, k, i, owner):
        return remote(
            grad_ref.at[a, owner, other[i]], near.at[a, k, i], send.at[a, k, i], recv.at[a, k, i], (flip(d, 1), m)
        )

    def mid_copy(a, k, i):
        return remote(
            near.at[a, k, 2 + i], mid.at[a, k, i], send.at[a, k, 4 + i], recv.at[a, k, 4 + i], (flip(d, second), m)
        )

    def far_copy(a, k):
        return remote(mid.at[a, k, 1], far.at[a, k], send.at[a, k, 6], recv.at[a, k, 6], (flip(d, first), m))

    def line_copy(a, k, owner):
        return remote(far.at[a, k], line.at[a, mp - k], send.at[a, k, 7], recv.at[a, mp - k, 7], (d, owner))

    def spread(a, i, piece, bit):
        ref = out_ref.at[a, piece]
        return remote(ref, ref, send.at[a, mp, i], recv.at[a, mp, i], (flip(d, bit), m))

    for a, k in units:
        for i in (2, 3, 0, 1):
            go(near_copy(a, k, i, lax.rem(m + k, mp)))
    for t in range(len(units) + 2):
        if t < len(units):
            a, k = units[t]
            owner = lax.rem(m + k, mp)
            for i in (2, 3, 0, 1):
                near_copy(a, k, i, owner).wait_recv()
                add(near.at[a, k, i], grad_ref.at[a, owner, mine[i]])
                if i >= 2:
                    go(mid_copy(a, k, i - 2))
        if 0 <= t - 1 < len(units):
            a, k = units[t - 1]
            for i in (1, 0):
                mid_copy(a, k, i).wait_recv()
                add(mid.at[a, k, i], near.at[a, k, i])
                if i:
                    go(far_copy(a, k))
        if 0 <= t - 2 < len(units):
            a, k = units[t - 2]
            far_copy(a, k).wait_recv()
            add(far.at[a, k], mid.at[a, k, 0])
            if k:
                go(line_copy(a, k, lax.rem(m + k, mp)))
    for a in range(BLOCKS):
        total = far[a, 0].astype(F32)
        for k in range(1, mp):
            remote(line.at[a, k], line.at[a, k], send.at[a, k, 7], recv.at[a, k, 7], (d, m)).wait_recv()
            total = total + line[a, k].astype(F32)
        out_ref[a, s] = total.astype(BF16)
        go(spread(a, 0, s, first))
        go(spread(a, 1, s, second))
        go(spread(a, 3, s, 1))
    for a in range(BLOCKS):
        spread(a, 0, s1, first).wait_recv()
        go(spread(a, 2, s1, second))
        go(spread(a, 4, s1, 1))
        spread(a, 1, s2, second).wait_recv()
        go(spread(a, 5, s2, 1))
    for a in range(BLOCKS):
        spread(a, 2, s3, second).wait_recv()
        go(spread(a, 6, s3, 1))
    for a in range(BLOCKS):
        for i, piece in ((3, s), (4, s1), (5, s2), (6, s3)):
            spread(a, i, flip(piece, 1), 1).wait_recv()
    for copy in sent:
        copy.wait_send()


def reduce_grads(grads, mp):
    blocks, _, inner, rows, width = grads.shape
    return pl.pallas_call(
        partial(reduce_kernel, mp),
        out_shape=jax.ShapeDtypeStruct((blocks, inner, rows, width), BF16),
        in_specs=[pl.BlockSpec(memory_space=pltpu.VMEM)],
        out_specs=pl.BlockSpec(memory_space=pltpu.VMEM),
        scratch_shapes=[
            pltpu.VMEM((blocks, mp, 4, rows, width), BF16),
            pltpu.VMEM((blocks, mp, 2, rows, width), BF16),
            pltpu.VMEM((blocks, mp, rows, width), BF16),
            pltpu.VMEM((blocks, mp, rows, width), BF16),
            pltpu.SemaphoreType.DMA((blocks, mp + 1, 8)),
            pltpu.SemaphoreType.DMA((blocks, mp + 1, 8)),
        ],
        input_output_aliases={},
        compiler_params=pltpu.CompilerParams(
            collective_id=1, has_side_effects=True, vmem_limit_bytes=63 * 1024 * 1024
        ),
    )(grads)


def norm_rows(hidden, gain_vec, shift_vec):
    row_mean = jnp.mean(hidden, axis=-1, keepdims=True)
    centred = hidden - row_mean
    variance = jnp.mean(centred * centred, axis=-1, keepdims=True)
    row_scale = lax.rsqrt(variance + EPS)
    normed = centred * row_scale
    return (normed * gain_vec + shift_vec, normed, row_scale)


def norm_back(grad_out, normed, row_scale, gain_vec):
    grad_normed = grad_out * gain_vec
    inner_mean = jnp.mean(grad_normed, axis=-1, keepdims=True)
    cross_mean = jnp.mean(grad_normed * normed, axis=-1, keepdims=True)
    grad_in = row_scale * (grad_normed - inner_mean - normed * cross_mean)
    return (grad_in, jnp.sum(grad_out * normed, axis=0), jnp.sum(grad_out, axis=0))


def on_device(
    token_block,
    token_offset,
    lengths,
    group_counts,
    table,
    weight_qkv,
    bias_query,
    bias_value,
    weight_out,
    bias_out,
    gain_one,
    shift_one,
    weight_in,
    bias_in,
    weight_down,
    bias_down,
    gain_two,
    shift_two,
    cotangent,
):
    axes = ("dp", "mp")
    devices = lax.axis_size(axes)
    mp = lax.axis_size("mp")
    dp = lax.axis_size("dp")
    me = lax.axis_index(axes)
    tok_rows = token_offset.shape[0]
    width = table.shape[1]
    sent_local = lengths.shape[0]
    shard_rows = weight_down.shape[0]
    qkv_rows = weight_qkv.shape[1]
    own_heads = qkv_rows // (3 * HD)
    heads = own_heads * mp
    slice_rows = shard_rows // INNER

    own = jnp.stack([jnp.concatenate([weight_qkv.T, weight_out], axis=0), weight_in, weight_down])
    whole = gather_weights(own.reshape(BLOCKS, INNER, slice_rows, width), mp)
    whole = whole.reshape(BLOCKS, mp, shard_rows, width)
    qkv_t = whole[0, :, :qkv_rows].reshape(heads * 3 * HD, width)
    w_out = whole[0, :, qkv_rows:].reshape(heads * HD, width)
    w_in = whole[1]
    w_down = whole[2]
    bias_all = lax.all_gather(jnp.concatenate([bias_query, bias_value, bias_in]), "mp", axis=0, tiled=False)
    b_query = bias_all[:, : own_heads * HD].reshape(heads, HD).astype(F32)
    b_value = bias_all[:, own_heads * HD : 2 * own_heads * HD].reshape(heads, HD).astype(F32)
    b_in = bias_all[:, 2 * own_heads * HD :].astype(F32)

    capacity = max(2, 2 * tok_rows // devices)
    token_owner = token_block[:, 0]
    owner_hits = (token_owner[:, None] == jnp.arange(devices, dtype=jnp.int32)[None, :]).astype(jnp.int32)
    slot_index = jnp.sum((jnp.cumsum(owner_hits, axis=0) - 1) * owner_hits, axis=1)
    slot_place = token_owner * capacity + slot_index
    requests = jnp.full((devices * capacity,), -1, jnp.int32).at[slot_place].set(token_offset)
    wanted = lax.all_to_all(requests.reshape(devices, capacity), axes, split_axis=0, concat_axis=0, tiled=True)
    slot_live = wanted >= 0
    wanted_rows = jnp.maximum(wanted, 0)
    fetched = lax.all_to_all(table[wanted_rows], axes, split_axis=0, concat_axis=0, tiled=True)
    embedded = fetched.reshape(devices * capacity, width)[slot_place]

    total_sent = sent_local * devices
    group_num = group_counts.shape[0]
    sent_index = me * sent_local + jnp.arange(sent_local, dtype=jnp.int32)
    offsets = jnp.cumsum(group_counts) - group_counts
    member = (sent_index[:, None] >= offsets[None, :]) & (sent_index[:, None] < (offsets + group_counts)[None, :])
    group_weight = total_sent / (group_num * group_counts.astype(F32))
    sent_weight = jnp.sum(jnp.where(member, group_weight[None, :], F32(0.0)), axis=1)
    positions = jnp.arange(SEQ, dtype=jnp.int32)
    token_live = (positions[None, :] < lengths[:, None]).astype(F32)
    row_weight = (token_live * sent_weight[:, None]).reshape(tok_rows)
    count_local = jnp.sum(lengths).astype(F32)

    dot = partial(jnp.einsum, preferred_element_type=F32)
    mixed = dot("td,cd->tc", embedded, qkv_t).reshape(sent_local, SEQ, heads, 3, HD)
    queries = (mixed[:, :, :, 0] + b_query).astype(BF16)
    key_rows = mixed[:, :, :, 1].astype(BF16)
    value_rows = (mixed[:, :, :, 2] + b_value).astype(BF16)
    scores = dot("sqhe,skhe->shqk", queries, key_rows) * 0.125
    valid = positions[None, :] < lengths[:, None]
    scores = jnp.where(valid[:, None, None, :], scores, F32(-1e30))
    probs = jax.nn.softmax(scores, axis=-1)
    probs_low = probs.astype(BF16)
    context = dot("shqk,skhe->sqhe", probs_low, value_rows).astype(BF16)
    context_rows = context.reshape(tok_rows, heads * HD)
    gain_one_f = gain_one.astype(F32)
    gain_two_f = gain_two.astype(F32)
    first_out, normed_one, scale_one = norm_rows(
        embedded.astype(F32) + dot("tc,cd->td", context_rows, w_out) + bias_out.astype(F32),
        gain_one_f,
        shift_one.astype(F32),
    )
    first_low = first_out.astype(BF16)
    hidden_pre = dot("td,mdf->tmf", first_low, w_in) + b_in
    gelu_val, gelu_pull = jax.vjp(partial(jax.nn.gelu, approximate=False), hidden_pre)
    hidden_act = gelu_val.astype(BF16)
    down_sum = dot("tmf,mfd->td", hidden_act, w_down)
    final_out, normed_two, scale_two = norm_rows(
        first_out + down_sum + bias_down.astype(F32), gain_two_f, shift_two.astype(F32)
    )
    activations = final_out.astype(BF16)
    grad_final = row_weight[:, None] * cotangent.astype(F32)
    grad_h2, grad_gain_two, grad_shift_two = norm_back(grad_final, normed_two, scale_two, gain_two_f)
    grad_bias_down = jnp.sum(grad_h2, axis=0)
    grad_down = grad_h2.astype(BF16)
    grad_w_down = dot("tmf,td->mfd", hidden_act, grad_down)
    grad_act = dot("td,mfd->tmf", grad_down, w_down)
    grad_pre = gelu_pull(grad_act)[0].astype(BF16)
    grad_bias_in = jnp.sum(grad_pre.astype(F32), axis=0)
    grad_w_in = dot("td,tmf->mdf", first_low, grad_pre)
    grad_first = grad_h2 + dot("tmf,mdf->td", grad_pre, w_in)
    grad_h1, grad_gain_one, grad_shift_one = norm_back(grad_first, normed_one, scale_one, gain_one_f)
    grad_bias_out = jnp.sum(grad_h1, axis=0)
    grad_attn = grad_h1.astype(BF16)
    grad_w_out = dot("tc,td->cd", context_rows, grad_attn)
    grad_context = dot("td,cd->tc", grad_attn, w_out).astype(BF16).reshape(sent_local, SEQ, heads, HD)
    grad_probs = dot("sqhe,skhe->shqk", grad_context, value_rows)
    grad_value = dot("shqk,sqhe->skhe", probs_low, grad_context).astype(BF16)
    grad_scores = (probs * (grad_probs - jnp.sum(grad_probs * probs, axis=-1, keepdims=True))).astype(BF16)
    grad_query = (dot("shqk,skhe->sqhe", grad_scores, key_rows) * 0.125).astype(BF16)
    grad_key = (dot("shqk,sqhe->skhe", grad_scores, queries) * 0.125).astype(BF16)
    grad_mixed = jnp.stack([grad_query, grad_key, grad_value], axis=3).reshape(tok_rows, heads * 3 * HD)
    grad_w_qkv = dot("tc,td->cd", grad_mixed, embedded)
    grad_bias_query = jnp.sum(grad_query.astype(F32), axis=(0, 1)).reshape(mp, own_heads * HD)
    grad_bias_value = jnp.sum(grad_value.astype(F32), axis=(0, 1)).reshape(mp, own_heads * HD)
    grad_embed = grad_h1 + dot("tc,cd->td", grad_mixed, qkv_t)

    grads = jnp.stack(
        [
            jnp.concatenate(
                [grad_w_qkv.reshape(mp, qkv_rows, width), grad_w_out.reshape(mp, own_heads * HD, width)], axis=1
            ),
            grad_w_in,
            grad_w_down,
        ]
    ).astype(BF16)
    summed = reduce_grads(grads.reshape(BLOCKS, mp, INNER, slice_rows, width), mp)
    group = summed
    for step in range(1, dp // INNER):
        shift = [(i, (i + step * INNER) % dp) for i in range(dp)]
        summed = (summed.astype(F32) + lax.ppermute(group, "dp", shift).astype(F32)).astype(BF16)
    summed = summed.reshape(BLOCKS, shard_rows, width)

    small = lax.psum(
        (
            count_local,
            grad_gain_one,
            grad_shift_one,
            grad_bias_out,
            grad_gain_two,
            grad_shift_two,
            grad_bias_down,
            grad_bias_query,
            grad_bias_value,
            grad_bias_in,
        ),
        axes,
    )
    factor = lax.rsqrt(small[0])
    gain_one_s, shift_one_s, bias_out_s, gain_two_s, shift_two_s, bias_down_s = (v * factor for v in small[1:7])
    m = lax.axis_index("mp")
    bias_query_s, bias_value_s, bias_in_s = (v[m] * factor for v in small[7:])

    outgoing = jnp.zeros((devices * capacity, width), BF16).at[slot_place].set(grad_embed.astype(BF16))
    incoming = lax.all_to_all(
        outgoing.reshape(devices, capacity, width), axes, split_axis=0, concat_axis=0, tiled=True
    )
    received = jnp.where(slot_live[..., None], incoming.astype(F32), F32(0.0)).reshape(devices * capacity, width)
    grad_table = jnp.zeros(table.shape, F32).at[wanted_rows.reshape(-1)].add(received * factor)
    scaled = summed.astype(F32) * factor
    return (
        activations,
        grad_table,
        scaled[0, :qkv_rows].T,
        bias_query_s,
        bias_value_s,
        scaled[0, qkv_rows:],
        bias_out_s,
        gain_one_s,
        shift_one_s,
        scaled[1],
        bias_in_s,
        scaled[2],
        bias_down_s,
        gain_two_s,
        shift_two_s,
    )


def solution(mesh):
    placed = (
        P(("dp", "mp"), None),
        P(("dp", "mp")),
        P(("dp", "mp")),
        P(),
        P(("dp", "mp"), None),
        P(None, "mp"),
        P("mp"),
        P("mp"),
        P("mp", None),
        P(),
        P(),
        P(),
        P(None, "mp"),
        P("mp"),
        P("mp", None),
        P(),
        P(),
        P(),
        P(("dp", "mp"), None),
    )
    return jax.shard_map(
        on_device,
        mesh=mesh,
        in_specs=placed,
        out_specs=(
            P(("dp", "mp"), None),
            P(("dp", "mp"), None),
            P(None, "mp"),
            P("mp"),
            P("mp"),
            P("mp", None),
            P(),
            P(),
            P(),
            P(None, "mp"),
            P("mp"),
            P("mp", None),
            P(),
            P(),
            P(),
        ),
        check_vma=False,
    )
```

time: 697 us -> 433 us (0.62)
  waiting for transfers between devices: 368 us -> 10.5 us
  Pallas kernels: 0 us -> 166 us
  other arithmetic: 109 us -> 67.6 us
  blocking collectives: 76.3 us -> 49.6 us
  starting transfers between devices: 8.6 us -> 25.6 us
  between operations: 16.8 us -> 3.01 us
  matrix products: 51.5 us -> 42.8 us
    pallas_call x0 -> x2, Pallas kernels: none -> 166 us  [the longest x1 92.9 us: reduce_grads(): pl.pallas_call(partial(reduce_kernel, mp), out_shape=jax.ShapeDtypeStruct...]
    reduce_scatter x4 -> x0, waiting for transfers between devices: 164 us -> none  [the longest x1 59.9 us: on_device(): lax.psum_scatter(jnp.einsum('rf,df->rd', grad_pre, weight_in, preferred_e...]
    all_gather x4 -> x0, waiting for transfers between devices: 132 us -> none  [the longest x1 36.5 us: on_device(): lax.all_gather(grad_h2.astype(bf16), 'mp', axis=0, tiled=True)]
    psum x1 -> x0, waiting for transfers between devices: 51.8 us -> none  [on_device(): lax.psum(grad_weight_qkv.astype(jnp.bfloat16), 'dp').astype(jnp.float32)]
    mul x14 -> x11, other arithmetic: 46 us -> 10.2 us  [the longest x6 3.57 us: on_device(): v * factor]
    all_to_all x2 -> x3, starting transfers between devices: 7.84 us -> 25.6 us  [the longest x1 13.5 us: on_device(): lax.all_to_all(table[wanted_rows], axes, split_axis=0, concat_axis=0, til...]
    slice x4 -> x5, local copies, waits for them, and re-layouts: 1.26 us -> 16.2 us  [the longest x1 8.07 us: on_device(): w_down = whole[2]]
    all_to_all x1 -> x0, blocking collectives: 13.6 us -> none  [on_device(): lax.all_to_all(requests.reshape(devices, capacity), ('dp', 'mp'), split_a...]
  transfers between devices with their start and end apart: 11 -> 3, of which waited for: 9 -> 1; matrix products, arithmetic and copies ran while one was open for 7% -> 10% of each run, Pallas kernels for 0% -> 39%
where the time goes in v1:
time: 433 us; the launch traced here: 426 us
  Pallas kernels  166 us (38%)
  other arithmetic  67.6 us (16%)
  local copies, waits for them, and re-layouts  60.6 us (14%)
  blocking collectives  49.6 us (11%)
  matrix products  42.8 us (10%)
  starting transfers between devices  25.6 us (6%)
  waiting for transfers between devices  10.5 us (2%)
    pallas_call x1, Pallas kernels, reduce_grads(): pl.pallas_call(partial(reduce_kernel, mp), out_shape=jax.ShapeDtypeStruct...  92.9 us
    pallas_call x1, Pallas kernels, gather_weights(): pl.pallas_call(partial(gather_kernel, mp), out_shape=jax.ShapeDtypeStruct...  73.1 us
    psum x1, blocking collectives, on_device(): lax.psum((count_local, grad_gain_one, grad_shift_one, grad_bias_out, grad...  39.1 us
    scatter-add x1, other arithmetic, on_device(): jnp.zeros(table.shape, F32).at[wanted_rows.reshape(-1)]  23.7 us
    gather x1, local copies, waits for them, and re-layouts, on_device(): table[wanted_rows]  14 us
    all_to_all x1, starting transfers between devices, on_device(): lax.all_to_all(table[wanted_rows], axes, split_axis=0, concat_axis=0, til...  13.5 us
    all_to_all x1, waiting for transfers between devices, on_device(): lax.all_to_all(table[wanted_rows], axes, split_axis=0, concat_axis=0, til...  10.5 us
    all_gather x1, blocking collectives, on_device(): lax.all_gather(jnp.concatenate([bias_query, bias_value, bias_in]), 'mp',...  10.5 us
  transfers between devices with their start and end apart: 3, of which 1 were waited for; matrix products, arithmetic and copies ran while one was open for 10% of the time, Pallas kernels for 39%

profile of v1, /device:TPU:1, one launch (start us, length us, event | category | flops | bytes accessed | tf_op | source)
XLA Modules:
  0.0 425.7 jit_solution(1981399910635764632)
XLA Ops:
  6.0 7.1 %all-to-all-start = ((s32[32,1,16]{2,1,0:T(1,128)}), s32[32,1,16]{2,1,0:T(1,128)S(1)}, u32[]{:S(2)}, u32[]{:S(2)}) async-start(s32[32,1,16]{2,1,0:T(1,128)} %bitcast.5), calls=%async_computation | async-start | bytes 32768 | tf_op jit(solution)/shard_map/all_to_all | solution.py:309
  15.9 10.5 %all-gather.1 = bf16[4,1,1152]{2,1,0:T(2,128)(2,1)S(1)} all-gather(bf16[1,1,1152]{2,1,0:T(2,128)(2,1)S(1)} %reshape.350), channel_id=2, replica_groups=mesh['dp'=8,'mp'=4] {'mp'}, dimensions={0}, use_global_device_ids=true | all-gather | bytes 11520 | tf_op jit(solution)/shard_map/all_gather | solution.py:298
  31.7 73.1 %shard_map.298 = bf16[3,4,8,96,768]{4,3,2,1,0:T(8,128)(2,1)} custom-call(bf16[3,8,96,768]{3,2,1,0:T(8,128)(2,1)} %pad_maximum_fusion.2.own_ref), custom_call_target="tpu_custom_call" | custom-call | tf_op jit(solution)/shard_map/pallas_call | solution.py:111
  106.2 4.1 slice.74
  114.4 14.0 %gather_fusion = bf16[512,768]{1,0:T(8,128)(2,1)} fusion(bf16[15664,768]{1,0:T(8,128)(2,1)} %param.23, s32[1024]{0:T(1024)S(1)} %pad_clamp_fusion.1), kind=kCustom, calls=%fused_computation | custom fusion | bytes 1574912 | tf_op jit(solution)/shard_map/gather | solution.py:312
  128.5 13.5 %all-to-all-start.1 = ((bf16[32,16,768]{2,1,0:T(8,128)(2,1)}), bf16[32,16,768]{2,1,0:T(8,128)(2,1)S(1)}, u32[]{:S(2)}, u32[]{:S(2)}) async-start(bf16[32,16,768]{2,1,0:T(8,128)(2,1)} %bitcast.6), calls=%async_computation.1 | async-start | bytes 1572864 | tf_op jit(solution)/shard_map/all_to_all | solution.py:312
  143.4 8.1 %fusion.62 = (bf16[1,4,8,96,768]{4,3,2,1,0:T(8,128)(2,1)}, bf16[1,4,8,96,768]{4,3,2,1,0:T(8,128)(2,1)}) fusion(bf16[3,4,8,96,768]{4,3,2,1,0:T(8,128)(2,1)} %shard_map.298), kind=kLoop, calls=%fused_computation.155 | loop fusion | bytes 18874368 | tf_op jit(solution)/shard_map/slice | solution.py:297
  152.1 10.5 %all-to-all-done.1 = bf16[32,16,768]{2,1,0:T(8,128)(2,1)S(1)} async-done(((bf16[32,16,768]{2,1,0:T(8,128)(2,1)}), bf16[32,16,768]{2,1,0:T(8,128)(2,1)S(1)}, u32[]{:S(2)}, u32[]{:S(2)}) %all-to-all-start.1) | async-done | bytes 786464 | tf_op jit(solution)/shard_map/all_to_all | solution.py:312
  163.9 4.1 fusion.67
  170.6 3.0 fusion.15
  179.8 4.6 %fusion.27 = (u8[256,768]{1,0:T(8,128)(4,1)S(1)}, u8[256,768]{1,0:T(8,128)(4,1)S(1)}, f32[256,4,768]{2,0,1:T(8,128)S(1)}) fusion(f32[4,768]{1,0:T(4,128)S(1)} %copy-done.17, bf16[4,768,768]{2,1,0:T(8,128)(2,1)} %bitcast.185, f32[256,768]{1,0:T(8,128)S(1)} %get-tuple-element.51, f32[768]{0:T(1024)S(1)} %copy-done.24, f32[768]{0:T(1024)S(1)} %convert_element_type.154, ...), kind=kOutput, calls=%fused_computation.89 | convolution fusion | flops 1219559424 | bytes 9064448 | tf_op jit(solution)/shard_map/td,mdf->tmf/dot_general | solution.py:347
  184.4 7.7 %multiply_convert_fusion = (bf16[256,4,768]{2,0,1:T(8,128)(2,1)S(1)}, f32[256,4,768]{2,0,1:T(8,128)S(1)}) fusion(f32[256,4,768]{2,0,1:T(8,128)S(1)} %get-tuple-element.52, f32[4,768]{1,0:T(4,128)S(1)} %copy-done.17, u8[256,768]{1,0:T(8,128)(4,1)S(1)} %get-tuple-element.16, u8[256,768]{1,0:T(8,128)(4,1)S(1)} %get-tuple-element.15), kind=kLoop, calls=%fused_computation.21 | loop fusion | flops 55836672 | bytes 8269824 | tf_op jit(solution)/shard_map/convert_element_type | solution.py:349
  203.2 3.6 convert_reduce_fusion.1
  213.2 3.7 convolution_convert_fusion.1
  216.9 3.8 convolution_convert_fusion
  223.6 3.2 copy.113
  226.9 4.6 %reshape.300 = bf16[256,2304]{0,1:T(8,128)(2,1)} reshape(bf16[4,64,12,3,64]{1,0,4,3,2:T(4,128)(2,1)} %copy.113) | data formatting | bytes 2359296 | tf_op jit(solution)/shard_map/reshape | solution.py:375
  232.1 39.1 %all-reduce = (f32[]{:T(128)}, f32[4,192]{1,0:T(4,128)S(1)}, f32[4,192]{1,0:T(4,128)}, f32[768]{0:T(1024)S(1)}, f32[768]{0:T(1024)S(1)}, /*index=5*/f32[768]{0:T...) all-reduce(f32[]{:T(128)S(6)} %convert_element_type.178, ...), channel_id=1, replica_groups=mesh['dp'=8,'mp'=4] {'dp','mp'}, use_global_device_ids=true, to_apply=%region_19.20 | all-reduce | flops 9217 | bytes 73736 | tf_op jit(solution)/shard_map/psum | solution.py:397
  276.6 4.3 %fusion.21 = bf16[256,768]{1,0:T(8,128)(2,1)} fusion(f32[256,768]{1,0:T(8,128)S(1)} %get-tuple-element.38, bf16[256,2304]{0,1:T(8,128)(2,1)} %reshape.300, bf16[2304,768]{1,0:T(8,128)(2,1)} %bitcast.194), kind=kOutput, calls=%fused_computation.69 | convolution fusion | flops 906362880 | bytes 5898240 | tf_op jit(solution)/shard_map/tc,cd->td/dot_general | solution.py:379
  280.9 3.2 scatter_custom_fusion.1
  284.0 5.0 %all-to-all-start.2 = ((bf16[32,16,768]{2,1,0:T(8,128)(2,1)}), bf16[32,16,768]{2,1,0:T(8,128)(2,1)}, u32[]{:S(2)}, u32[]{:S(2)}) async-start(bf16[32,16,768]{2,1,0:T(8,128)(2,1)} %bitcast.197), calls=%async_computation.2 | async-start | bytes 1572864 | tf_op jit(solution)/shard_map/all_to_all | solution.py:418
  292.9 5.8 %pad_maximum_fusion.grad_ref = bf16[3,4,8,96,768]{4,3,2,1,0:T(8,128)(2,1)} fusion(bf16[1,4,8,96,768]{4,3,2,1,0:T(8,128)(2,1)S(1)} %bitcast.177, bf16[1,4,8,96,768]{4,3,2,1,0:T(8,128)(2,1)S(1)} %bitcast.174, bf16[1,4,8,96,768]{4,3,2,1,0:T(8,128)(2,1)S(1)} %bitcast.178), kind=kLoop, calls=%fused_computation.8 | loop fusion | flops 14155776 | bytes 28311552 | tf_op jit(solution)/shard_map/stack | solution.py:381
  298.7 92.9 %shard_map.299 = bf16[3,8,96,768]{3,2,1,0:T(8,128)(2,1)} custom-call(bf16[3,4,8,96,768]{4,3,2,1,0:T(8,128)(2,1)} %pad_maximum_fusion.grad_ref), custom_call_target="tpu_custom_call" | custom-call | tf_op jit(solution)/shard_map/pallas_call | solution.py:219
  401.7 23.7 %scatter_custom_fusion.2 = f32[15664,768]{1,0:T(8,128)} fusion(s32[512]{0:T(512)} %copy-done.33, f32[512,768]{1,0:T(8,128)S(1)} %bitcast.201, f32[]{:T(128)} %constant.54.clone.1), kind=kCustom, calls=%fused_computation.6 | custom fusion | flops 393216 | bytes 48120320 | tf_op jit(solution)/shard_map/scatter-add | solution.py:422
  (212 shorter events, 69.6 us)
Async XLA Ops:
  0.6 28.9 %copy-start.13 = (bf16[768,768]{1,0:T(8,128)(2,1)S(1)}, bf16[768,768]{1,0:T(8,128)(2,1)}, u32[]{:S(2)}) copy-start(bf16[768,768]{1,0:T(8,128)(2,1)} %param.33) | copy-start | bytes 3538948
  0.7 28.9 %copy-start.14 = (bf16[768,768]{1,0:T(8,128)(2,1)S(1)}, bf16[768,768]{1,0:T(8,128)(2,1)}, u32[]{:S(2)}) copy-start(bf16[768,768]{1,0:T(8,128)(2,1)} %param.31) | copy-start | bytes 3538948
  3.8 138.9 %copy-start.38 = (s32[256,1]{0,1:T(1,128)}, s32[256,1]{0,1:T(1,128)S(1)}, u32[]{:S(2)}) copy-start(s32[256,1]{0,1:T(1,128)S(1)} %compare_select_fusion) | copy-start | bytes 3076
  6.0 108.2 %all-to-all-start = ((s32[32,1,16]{2,1,0:T(1,128)}), s32[32,1,16]{2,1,0:T(1,128)S(1)}, u32[]{:S(2)}, u32[]{:S(2)}) async-start(s32[32,1,16]{2,1,0:T(1,128)} %bitcast.5), calls=%async_computation | async-start | bytes 32768 | tf_op jit(solution)/shard_map/all_to_all | solution.py:309
  106.2 5.4 %copy-start.40 = (bf16[768]{0:T(1024)(128)(2,1)S(1)}, bf16[768]{0:T(1024)(128)(2,1)}, u32[]{:S(2)}) copy-start(bf16[768]{0:T(1024)(128)(2,1)} %param.29) | copy-start | bytes 4612
  106.2 5.4 %copy-start.41 = (bf16[768]{0:T(1024)(128)(2,1)S(1)}, bf16[768]{0:T(1024)(128)(2,1)}, u32[]{:S(2)}) copy-start(bf16[768]{0:T(1024)(128)(2,1)} %param.30) | copy-start | bytes 4612
  106.2 6.0 %copy-start.42 = (bf16[768]{0:T(1024)(128)(2,1)S(1)}, bf16[768]{0:T(1024)(128)(2,1)}, u32[]{:S(2)}) copy-start(bf16[768]{0:T(1024)(128)(2,1)} %param.35) | copy-start | bytes 4612
  106.2 6.0 %copy-start.43 = (bf16[768]{0:T(1024)(128)(2,1)S(1)}, bf16[768]{0:T(1024)(128)(2,1)}, u32[]{:S(2)}) copy-start(bf16[768]{0:T(1024)(128)(2,1)} %param.28) | copy-start | bytes 4612
  106.2 6.6 %copy-start.44 = (bf16[768]{0:T(1024)(128)(2,1)S(1)}, bf16[768]{0:T(1024)(128)(2,1)}, u32[]{:S(2)}) copy-start(bf16[768]{0:T(1024)(128)(2,1)} %param.34) | copy-start | bytes 4612
  106.2 7.2 %copy-start.45 = (bf16[768]{0:T(1024)(128)(2,1)S(1)}, bf16[768]{0:T(1024)(128)(2,1)}, u32[]{:S(2)}) copy-start(bf16[768]{0:T(1024)(128)(2,1)} %param.36) | copy-start | bytes 4612
  114.2 56.5 %copy-start.34 = (f32[12,64]{1,0:T(8,128)}, f32[12,64]{1,0:T(8,128)S(1)}, u32[]{:S(2)}) copy-start(f32[12,64]{1,0:T(8,128)S(1)} %reshape.304) | copy-start | bytes 9220
  114.4 14.0 %copy-start.33 = (s32[512]{0:T(512)}, s32[512]{0:T(512)S(1)}, u32[]{:S(2)}) copy-start(s32[512]{0:T(512)S(1)} %reshape.308) | copy-start | bytes 6148
  128.5 34.2 %all-to-all-start.1 = ((bf16[32,16,768]{2,1,0:T(8,128)(2,1)}), bf16[32,16,768]{2,1,0:T(8,128)(2,1)S(1)}, u32[]{:S(2)}, u32[]{:S(2)}) async-start(bf16[32,16,768]{2,1,0:T(8,128)(2,1)} %bitcast.6), calls=%async_computation.1 | async-start | bytes 1572864 | tf_op jit(solution)/shard_map/all_to_all | solution.py:312
  163.9 14.3 %copy-start.6 = (bf16[256,768]{1,0:T(8,128)(2,1)}, bf16[256,768]{1,0:T(8,128)(2,1)S(1)}, u32[]{:S(2)}) copy-start(bf16[256,768]{1,0:T(8,128)(2,1)S(1)} %gather_fusion.1) | copy-start | bytes 1179652
  179.5 22.3 %copy-start.19 = (f32[256]{0:T(256)}, f32[256]{0:T(256)S(1)}, u32[]{:S(2)}) copy-start(f32[256]{0:T(256)S(1)} %broadcast_multiply_fusion.11) | copy-start | bytes 3076
  179.5 12.6 %slice-start.8 = ((s8[4718592]{0:T(1024)(128)(4,1)}), s8[4194304]{0:T(1024)(128)(4,1)S(1)}, s32[]{:S(2)}) async-start(s8[4718592]{0:T(1024)(128)(4,1)} %bitcast.189), calls=%async_computation.11 | async-start | bytes 8388608
  179.7 22.0 %copy-start.30 = (f32[256]{0:T(256)}, f32[256]{0:T(256)S(1)}, u32[]{:S(2)}) copy-start(f32[256]{0:T(256)S(1)} %add_rsqrt_fusion.1) | copy-start | bytes 3076
  179.8 12.3 %slice-start.9 = ((s8[4718592]{0:T(1024)(128)(4,1)}), s8[524288]{0:T(1024)(128)(4,1)S(1)}, s32[]{:S(2)}) async-start(s8[4718592]{0:T(1024)(128)(4,1)} %bitcast.189), calls=%async_computation.12 | async-start | bytes 1048576
  184.4 7.7 %copy-start.39 = (f32[768]{0:T(1024)S(1)}, f32[768]{0:T(1024)}, u32[]{:S(2)}) copy-start(f32[768]{0:T(1024)} %convert_element_type.159) | copy-start | bytes 9220
  226.9 5.1 %copy-start.29 = (f32[4,768]{1,0:T(4,128)S(1)}, f32[4,768]{1,0:T(4,128)}, u32[]{:S(2)}) copy-start(f32[4,768]{1,0:T(4,128)} %get-tuple-element.62) | copy-start | bytes 36868
  226.9 5.1 %copy-start.36 = (f32[768]{0:T(1024)S(1)}, f32[768]{0:T(1024)}, u32[]{:S(2)}) copy-start(f32[768]{0:T(1024)} %get-tuple-element.17) | copy-start | bytes 9220
  276.6 12.4 %copy-start.7 = (bf16[256,768]{1,0:T(8,128)(2,1)S(1)}, bf16[256,768]{1,0:T(8,128)(2,1)}, u32[]{:S(2)}) copy-start(bf16[256,768]{1,0:T(8,128)(2,1)} %copy-done.6) | copy-start | bytes 1179652
  280.9 8.2 %copy-start.5 = (bf16[256,2304]{0,1:T(8,128)(2,1)S(1)}, bf16[256,2304]{0,1:T(8,128)(2,1)}, u32[]{:S(2)}) copy-start(bf16[256,2304]{0,1:T(8,128)(2,1)} %reshape.300) | copy-start | bytes 3538948
  284.0 116.3 %all-to-all-start.2 = ((bf16[32,16,768]{2,1,0:T(8,128)(2,1)}), bf16[32,16,768]{2,1,0:T(8,128)(2,1)}, u32[]{:S(2)}, u32[]{:S(2)}) async-start(bf16[32,16,768]{2,1,0:T(8,128)(2,1)} %bitcast.197), calls=%async_computation.2 | async-start | bytes 1572864 | tf_op jit(solution)/shard_map/all_to_all | solution.py:418
  (36 other events, 119.6 us)

commit v2 on v1

--- a/solution.py
+++ b/solution.py
@@ -31,12 +31,38 @@
     return d + bit - 2 * bit * lax.rem(lax.div(d, bit), 2)
 
 
-def enter(d, m, mp):
+def place(a, owner, piece, mp):
+    if a == 0:
+        return lax.div(piece, 2) * (2 * mp) + owner * 2 + lax.rem(piece, 2)
+    return owner * INNER + piece
+
+
+def nearest(m, mp):
+    table = []
+    for at in range(mp):
+        owners = sorted((abs(o - at), o < at, (o - at) % mp) for o in range(mp) if o != at)
+        table.append([entry[2] for entry in owners])
+    offsets = []
+    for i in range(mp - 1):
+        k = table[0][i]
+        for at in range(1, mp):
+            k = jnp.where(m == at, table[at][i], k)
+        offsets.append(k)
+    return offsets
+
+
+def enter_all(me, mp, devices):
     barrier = pltpu.get_barrier_semaphore()
-    peers = [(flip(d, bit), m) for bit in (1, 2, 4)] + [(d, lax.rem(m + k, mp)) for k in range(1, mp)]
-    for peer in peers:
-        pl.semaphore_signal(barrier, inc=1, device_id=peer, device_id_type=MESH)
-    pl.semaphore_wait(barrier, len(peers))
+
+    def greet(j, _):
+        peer = lax.rem(me + j, devices)
+        pl.semaphore_signal(
+            barrier, inc=1, device_id=(lax.div(peer, mp), lax.rem(peer, mp)), device_id_type=MESH
+        )
+        return 0
+
+    lax.fori_loop(1, devices, greet, 0)
+    pl.semaphore_wait(barrier, devices - 1)
 
 
 def remote(src, dst, send, recv, peer):
@@ -45,88 +71,229 @@
     )
 
 
-def gather_kernel(mp, own_ref, out_ref, send, recv, own_sem):
+def row_exchange(me, mp, devices, rows_ref, rows_out, send, recv, own_sem):
+    def copy_to(j):
+        peer = lax.rem(me + j, devices)
+        return remote(
+            rows_ref.at[peer], rows_out.at[me], send.at[j], recv.at[j], (lax.div(peer, mp), lax.rem(peer, mp))
+        )
+
+    def start():
+        pltpu.make_async_copy(rows_ref.at[me], rows_out.at[me], own_sem).start()
+
+        def body(j, _):
+            copy_to(j).start()
+            return 0
+
+        lax.fori_loop(1, devices, body, 0)
+
+    def finish():
+        pltpu.make_async_copy(rows_ref.at[me], rows_out.at[me], own_sem).wait()
+
+        def body(j, _):
+            peer = lax.rem(me + devices - j, devices)
+            back = remote(
+                rows_ref.at[peer], rows_out.at[peer], send.at[j], recv.at[j], (lax.div(peer, mp), lax.rem(peer, mp))
+            )
+            back.wait_recv()
+            back.wait_send()
+            return 0
+
+        lax.fori_loop(1, devices, body, 0)
+
+    return start, finish
+
+
+def gather_kernel(
+    mp, devices, own_ref, bias_ref, rows_ref, out_ref, bias_out, rows_out, send, recv, z_send, own_sem, b_send, b_recv, r_send, r_recv
+):
     d, m, first, second = position()
-    enter(d, m, mp)
+    me = d * mp + m
+    enter_all(me, mp, devices)
     s = lax.rem(d, INNER)
     s1 = flip(s, first)
     s2 = flip(s, second)
     s3 = flip(s1, second)
+    above = jnp.minimum(m + 1, mp - 1)
+    below = jnp.maximum(m - 1, 0)
+
+    def z_copy(a, owner, to, slot):
+        at = out_ref.at[a, place(a, owner, s, mp)]
+        k = lax.rem(owner - to + mp, mp)
+        return remote(at, at, z_send.at[a, slot], recv.at[a, k, 0], (d, to))
+
+    def own_z(a, to, slot):
+        at = out_ref.at[a, place(a, m, s, mp)]
+        k = lax.rem(m - to + mp, mp)
+        return remote(own_ref.at[a, s], at, z_send.at[a, slot], recv.at[a, k, 0], (d, to))
+
+    def start_own(a):
+        @pl.when(m < mp - 1)
+        def _():
+            own_z(a, above, 0).start()
+
+        @pl.when(m > 0)
+        def _():
+            own_z(a, below, 1).start()
+
+    def own_copy(a, piece):
+        return pltpu.make_async_copy(own_ref.at[a, piece], out_ref.at[a, place(a, m, piece, mp)], own_sem.at[a, piece])
+
+    def bias_copy(k):
+        return remote(bias_ref, bias_out.at[m], b_send.at[k], b_recv.at[mp - k], (d, lax.rem(m + k, mp)))
+
+    start_rows, finish_rows = row_exchange(me, mp, devices, rows_ref, rows_out, r_send, r_recv, own_sem.at[BLOCKS, 0])
+    for k in range(1, mp):
+        bias_copy(k).start()
+    bias_own = pltpu.make_async_copy(bias_ref, bias_out.at[m], own_sem.at[BLOCKS, 1])
+    bias_own.start()
+    start_own(0)
+    start_rows()
+    for a in range(1, BLOCKS):
+        start_own(a)
     for a in range(BLOCKS):
-        pltpu.make_async_copy(own_ref.at[a], out_ref.at[a, m], own_sem.at[a]).start()
-    z_copies = []
-    for a in range(BLOCKS):
-        for k in range(1, mp):
-            copy = remote(
-                own_ref.at[a, s], out_ref.at[a, m, s], send.at[a, k, 0], recv.at[a, mp - k, 0], (d, lax.rem(m + k, mp))
-            )
-            copy.start()
-            z_copies.append(copy)
+        for piece in range(INNER):
+            own_copy(a, piece).start()
 
     def hop(a, k, piece, slot, bit):
-        ref = out_ref.at[a, lax.rem(m + k, mp), piece]
+        ref = out_ref.at[a, place(a, lax.rem(m + k, mp), piece, mp)]
         return remote(ref, ref, send.at[a, k, slot], recv.at[a, k, slot], (flip(d, bit), m))
 
-    units = [(a, k) for a in range(BLOCKS) for k in range(1, mp)]
+    offsets = nearest(m, mp)
+    units = [(a, i) for a in range(BLOCKS) for i in range(mp - 1)]
     sent = []
 
     def go(copy):
         copy.start()
         sent.append(copy)
 
-    def wait_z(a, k):
-        ref = out_ref.at[a, lax.rem(m + k, mp), s]
-        remote(ref, ref, send.at[a, k, 0], recv.at[a, k, 0], (d, lax.rem(m + k, mp))).wait_recv()
+    def z_forward(a, i):
+        owner = lax.rem(m + offsets[i], mp)
+        return owner, z_copy(a, owner, below, 2 + i), z_copy(a, owner, above, 2 + i)
 
     for t in range(len(units) + 3):
         if t < len(units):
-            a, k = units[t]
-            wait_z(a, k)
+            a, i = units[t]
+            k = offsets[i]
+            owner, down, up = z_forward(a, i)
+            remote(own_ref.at[a, s], out_ref.at[a, place(a, owner, s, mp)], send.at[a, k, 0], recv.at[a, k, 0], (d, owner)).wait_recv()
+
+            @pl.when(jnp.logical_and(owner > m, m > 0))
+            def _():
+                down.start()
+
+            @pl.when(jnp.logical_and(owner < m, m < mp - 1))
+            def _():
+                up.start()
+
             go(hop(a, k, s, 1, first))
             go(hop(a, k, s, 2, second))
             go(hop(a, k, s, 4, 1))
         if 0 <= t - 1 < len(units):
-            a, k = units[t - 1]
+            a, i = units[t - 1]
+            k = offsets[i]
             hop(a, k, s1, 1, first).wait_recv()
             go(hop(a, k, s1, 3, second))
             go(hop(a, k, s1, 5, 1))
         if 0 <= t - 2 < len(units):
-            a, k = units[t - 2]
+            a, i = units[t - 2]
+            k = offsets[i]
             hop(a, k, s2, 2, second).wait_recv()
             go(hop(a, k, s2, 6, 1))
             hop(a, k, s3, 3, second).wait_recv()
             go(hop(a, k, s3, 7, 1))
         if 0 <= t - 3 < len(units):
-            a, k = units[t - 3]
+            a, i = units[t - 3]
+            k = offsets[i]
             for slot, piece in ((4, s), (5, s1), (6, s2), (7, s3)):
                 hop(a, k, flip(piece, 1), slot, 1).wait_recv()
-    for copy in z_copies + sent:
+    finish_rows()
+    for k in range(1, mp):
+        remote(bias_ref, bias_out.at[lax.rem(m + k, mp)], b_send.at[k], b_recv.at[k], (d, lax.rem(m + k, mp))).wait_recv()
+        bias_copy(k).wait_send()
+    bias_own.wait()
+    for copy in sent:
         copy.wait_send()
     for a in range(BLOCKS):
-        pltpu.make_async_copy(own_ref.at[a], out_ref.at[a, m], own_sem.at[a]).wait()
-
-
-def gather_weights(own, mp):
-    _, inner, rows, width = own.shape
+        for piece in range(INNER):
+            own_copy(a, piece).wait()
+
+        @pl.when(m < mp - 1)
+        def _():
+            own_z(a, above, 0).wait_send()
+
+        @pl.when(m > 0)
+        def _():
+            own_z(a, below, 1).wait_send()
+
+        for i in range(mp - 1):
+            owner, down, up = z_forward(a, i)
+
+            @pl.when(jnp.logical_and(owner > m, m > 0))
+            def _():
+                down.wait_send()
+
+            @pl.when(jnp.logical_and(owner < m, m < mp - 1))
+            def _():
+                up.wait_send()
+
+
+def gather_weights(own, bias, rows, mp):
+    _, inner, piece_rows, width = own.shape
+    devices = rows.shape[0]
+    vmem = pl.BlockSpec(memory_space=pltpu.VMEM)
+    dma = pltpu.SemaphoreType.DMA
     return pl.pallas_call(
-        partial(gather_kernel, mp),
-        out_shape=jax.ShapeDtypeStruct((BLOCKS, mp, inner, rows, width), BF16),
-        in_specs=[pl.BlockSpec(memory_space=pltpu.VMEM)],
-        out_specs=pl.BlockSpec(memory_space=pltpu.VMEM),
+        partial(gather_kernel, mp, devices),
+        out_shape=(
+            jax.ShapeDtypeStruct((BLOCKS, mp * inner, piece_rows, width), BF16),
+            jax.ShapeDtypeStruct((mp, *bias.shape), BF16),
+            jax.ShapeDtypeStruct(rows.shape, BF16),
+        ),
+        in_specs=[vmem] * 3,
+        out_specs=(vmem,) * 3,
         scratch_shapes=[
-            pltpu.SemaphoreType.DMA((BLOCKS, mp, 8)),
-            pltpu.SemaphoreType.DMA((BLOCKS, mp, 8)),
-            pltpu.SemaphoreType.DMA((BLOCKS,)),
+            dma((BLOCKS, mp, 8)),
+            dma((BLOCKS, mp, 8)),
+            dma((BLOCKS, 1 + mp)),
+            dma((BLOCKS + 1, INNER)),
+            dma((mp,)),
+            dma((mp,)),
+            dma((devices,)),
+            dma((devices,)),
         ],
         compiler_params=pltpu.CompilerParams(
             collective_id=0, has_side_effects=True, vmem_limit_bytes=60 * 1024 * 1024
         ),
-    )(own)
-
-
-def reduce_kernel(mp, grad_ref, out_ref, near, mid, far, line, send, recv):
+    )(own, bias, rows)
+
+
+def reduce_kernel(
+    mp,
+    devices,
+    grad_ref,
+    small_ref,
+    rows_ref,
+    out_ref,
+    small_out,
+    rows_out,
+    near,
+    mid,
+    far,
+    line,
+    part,
+    part_in,
+    send,
+    recv,
+    p_send,
+    p_recv,
+    r_send,
+    r_recv,
+    own_sem,
+):
     d, m, first, second = position()
-    enter(d, m, mp)
+    me = d * mp + m
+    enter_all(me, mp, devices)
     s = lax.rem(d, INNER)
     s1 = flip(s, first)
     s2 = flip(s, second)
@@ -146,7 +313,7 @@
 
     def near_copy(a, k, i, owner):
         return remote(
-            grad_ref.at[a, owner, other[i]], near.at[a, k, i], send.at[a, k, i], recv.at[a, k, i], (flip(d, 1), m)
+            grad_ref.at[a, place(a, owner, other[i], mp)], near.at[a, k, i], send.at[a, k, i], recv.at[a, k, i], (flip(d, 1), m)
         )
 
     def mid_copy(a, k, i):
@@ -164,16 +331,38 @@
         ref = out_ref.at[a, piece]
         return remote(ref, ref, send.at[a, mp, i], recv.at[a, mp, i], (flip(d, bit), m))
 
-    for a, k in units:
+    def part_copy(i):
+        source = small_ref if i == 0 else part.at[i - 1]
+        return remote(source, part_in.at[i], p_send.at[i], p_recv.at[i], (flip(d, 2**i), m))
+
+    def total_copy(k):
+        return remote(
+            part.at[2], part_in.at[3 + m], p_send.at[2 + k], p_recv.at[3 + m], (d, lax.rem(m + k, mp))
+        )
+
+    def part_step(i):
+        part_copy(i).wait_recv()
+        part[i] = (small_ref[...] if i == 0 else part[i - 1]) + part_in[i]
+        if i < 2:
+            go(part_copy(i + 1))
+        else:
+            for k in range(1, mp):
+                go(total_copy(k))
+
+    start_rows, finish_rows = row_exchange(me, mp, devices, rows_ref, rows_out, r_send, r_recv, own_sem.at[0])
+    go(part_copy(0))
+    for n, (a, k) in enumerate(units):
         for i in (2, 3, 0, 1):
             go(near_copy(a, k, i, lax.rem(m + k, mp)))
+        if n == 0:
+            start_rows()
     for t in range(len(units) + 2):
         if t < len(units):
             a, k = units[t]
             owner = lax.rem(m + k, mp)
             for i in (2, 3, 0, 1):
                 near_copy(a, k, i, owner).wait_recv()
-                add(near.at[a, k, i], grad_ref.at[a, owner, mine[i]])
+                add(near.at[a, k, i], grad_ref.at[a, place(a, owner, mine[i], mp)])
                 if i >= 2:
                     go(mid_copy(a, k, i - 2))
         if 0 <= t - 1 < len(units):
@@ -189,6 +378,8 @@
             add(far.at[a, k], mid.at[a, k, 0])
             if k:
                 go(line_copy(a, k, lax.rem(m + k, mp)))
+        if t in (2, 5, 8):
+            part_step(t // 3)
     for a in range(BLOCKS):
         total = far[a, 0].astype(F32)
         for k in range(1, mp):
@@ -204,9 +395,18 @@
         go(spread(a, 4, s1, 1))
         spread(a, 1, s2, second).wait_recv()
         go(spread(a, 5, s2, 1))
+    part_in[3 + m] = part[2]
+    for k in range(1, mp):
+        owner = lax.rem(m + k, mp)
+        remote(part.at[2], part_in.at[3 + owner], p_send.at[2 + k], p_recv.at[3 + owner], (d, owner)).wait_recv()
+    whole_sum = part_in[3]
+    for k in range(1, mp):
+        whole_sum = whole_sum + part_in[3 + k]
+    small_out[...] = whole_sum
     for a in range(BLOCKS):
         spread(a, 2, s3, second).wait_recv()
         go(spread(a, 6, s3, 1))
+    finish_rows()
     for a in range(BLOCKS):
         for i, piece in ((3, s), (4, s1), (5, s2), (6, s3)):
             spread(a, i, flip(piece, 1), 1).wait_recv()
@@ -214,26 +414,39 @@
         copy.wait_send()
 
 
-def reduce_grads(grads, mp):
-    blocks, _, inner, rows, width = grads.shape
+def reduce_grads(grads, small, rows, mp):
+    blocks, pieces, piece_rows, width = grads.shape
+    devices = rows.shape[0]
+    vmem = pl.BlockSpec(memory_space=pltpu.VMEM)
+    dma = pltpu.SemaphoreType.DMA
     return pl.pallas_call(
-        partial(reduce_kernel, mp),
-        out_shape=jax.ShapeDtypeStruct((blocks, inner, rows, width), BF16),
-        in_specs=[pl.BlockSpec(memory_space=pltpu.VMEM)],
-        out_specs=pl.BlockSpec(memory_space=pltpu.VMEM),
+        partial(reduce_kernel, mp, devices),
+        out_shape=(
+            jax.ShapeDtypeStruct((blocks, pieces // mp, piece_rows, width), BF16),
+            jax.ShapeDtypeStruct(small.shape, F32),
+            jax.ShapeDtypeStruct(rows.shape, BF16),
+        ),
+        in_specs=[vmem] * 3,
+        out_specs=(vmem,) * 3,
         scratch_shapes=[
-            pltpu.VMEM((blocks, mp, 4, rows, width), BF16),
-            pltpu.VMEM((blocks, mp, 2, rows, width), BF16),
-            pltpu.VMEM((blocks, mp, rows, width), BF16),
-            pltpu.VMEM((blocks, mp, rows, width), BF16),
-            pltpu.SemaphoreType.DMA((blocks, mp + 1, 8)),
-            pltpu.SemaphoreType.DMA((blocks, mp + 1, 8)),
+            pltpu.VMEM((blocks, mp, 4, piece_rows, width), BF16),
+            pltpu.VMEM((blocks, mp, 2, piece_rows, width), BF16),
+            pltpu.VMEM((blocks, mp, piece_rows, width), BF16),
+            pltpu.VMEM((blocks, mp, piece_rows, width), BF16),
+            pltpu.VMEM((3, *small.shape), F32),
+            pltpu.VMEM((3 + mp, *small.shape), F32),
+            dma((blocks, mp + 1, 8)),
+            dma((blocks, mp + 1, 8)),
+            dma((2 + mp,)),
+            dma((3 + mp,)),
+            dma((devices,)),
+            dma((devices,)),
+            dma((1,)),
         ],
-        input_output_aliases={},
         compiler_params=pltpu.CompilerParams(
             collective_id=1, has_side_effects=True, vmem_limit_bytes=63 * 1024 * 1024
         ),
-    )(grads)
+    )(grads, small, rows)
 
 
 def norm_rows(hidden, gain_vec, shift_vec):
@@ -288,17 +501,11 @@
     heads = own_heads * mp
     slice_rows = shard_rows // INNER
 
-    own = jnp.stack([jnp.concatenate([weight_qkv.T, weight_out], axis=0), weight_in, weight_down])
-    whole = gather_weights(own.reshape(BLOCKS, INNER, slice_rows, width), mp)
-    whole = whole.reshape(BLOCKS, mp, shard_rows, width)
-    qkv_t = whole[0, :, :qkv_rows].reshape(heads * 3 * HD, width)
-    w_out = whole[0, :, qkv_rows:].reshape(heads * HD, width)
-    w_in = whole[1]
-    w_down = whole[2]
-    bias_all = lax.all_gather(jnp.concatenate([bias_query, bias_value, bias_in]), "mp", axis=0, tiled=False)
-    b_query = bias_all[:, : own_heads * HD].reshape(heads, HD).astype(F32)
-    b_value = bias_all[:, own_heads * HD : 2 * own_heads * HD].reshape(heads, HD).astype(F32)
-    b_in = bias_all[:, 2 * own_heads * HD :].astype(F32)
+    kinds = weight_qkv.reshape(width, own_heads, 3, HD).transpose(2, 1, 3, 0).reshape(qkv_rows, width)
+    own = jnp.stack([jnp.concatenate([kinds, weight_out], axis=0), weight_in, weight_down])
+    bias_own = jnp.concatenate([bias_query, bias_value, bias_in])
+    bias_rows = bias_own.shape[0] // 128
+    bias_own = jnp.pad(bias_own.reshape(bias_rows, 128), ((0, -bias_rows % 16), (0, 0)))
 
     capacity = max(2, 2 * tok_rows // devices)
     token_owner = token_block[:, 0]
@@ -309,8 +516,17 @@
     wanted = lax.all_to_all(requests.reshape(devices, capacity), axes, split_axis=0, concat_axis=0, tiled=True)
     slot_live = wanted >= 0
     wanted_rows = jnp.maximum(wanted, 0)
-    fetched = lax.all_to_all(table[wanted_rows], axes, split_axis=0, concat_axis=0, tiled=True)
+    whole, bias_all, fetched = gather_weights(
+        own.reshape(BLOCKS, INNER, slice_rows, width), bias_own, table[wanted_rows], mp
+    )
     embedded = fetched.reshape(devices * capacity, width)[slot_place]
+    w_query, w_key, w_value, w_out = whole[0].reshape(4, heads * HD, width)
+    w_in = whole[1].reshape(mp, shard_rows, width)
+    w_down = whole[2].reshape(mp, shard_rows, width)
+    bias_all = bias_all.reshape(mp, -1)
+    b_query = bias_all[:, : own_heads * HD].reshape(heads, HD).astype(F32)
+    b_value = bias_all[:, own_heads * HD : 2 * own_heads * HD].reshape(heads, HD).astype(F32)
+    b_in = bias_all[:, 2 * own_heads * HD : 2 * own_heads * HD + bias_in.shape[0]].astype(F32)
 
     total_sent = sent_local * devices
     group_num = group_counts.shape[0]
@@ -325,10 +541,10 @@
     count_local = jnp.sum(lengths).astype(F32)
 
     dot = partial(jnp.einsum, preferred_element_type=F32)
-    mixed = dot("td,cd->tc", embedded, qkv_t).reshape(sent_local, SEQ, heads, 3, HD)
-    queries = (mixed[:, :, :, 0] + b_query).astype(BF16)
-    key_rows = mixed[:, :, :, 1].astype(BF16)
-    value_rows = (mixed[:, :, :, 2] + b_value).astype(BF16)
+    by_head = (sent_local, SEQ, heads, HD)
+    queries = (dot("td,cd->tc", embedded, w_query).reshape(by_head) + b_query).astype(BF16)
+    key_rows = dot("td,cd->tc", embedded, w_key).reshape(by_head).astype(BF16)
+    value_rows = (dot("td,cd->tc", embedded, w_value).reshape(by_head) + b_value).astype(BF16)
     scores = dot("sqhe,skhe->shqk", queries, key_rows) * 0.125
     valid = positions[None, :] < lengths[:, None]
     scores = jnp.where(valid[:, None, None, :], scores, F32(-1e30))
@@ -372,59 +588,52 @@
     grad_scores = (probs * (grad_probs - jnp.sum(grad_probs * probs, axis=-1, keepdims=True))).astype(BF16)
     grad_query = (dot("shqk,skhe->sqhe", grad_scores, key_rows) * 0.125).astype(BF16)
     grad_key = (dot("shqk,sqhe->skhe", grad_scores, queries) * 0.125).astype(BF16)
-    grad_mixed = jnp.stack([grad_query, grad_key, grad_value], axis=3).reshape(tok_rows, heads * 3 * HD)
-    grad_w_qkv = dot("tc,td->cd", grad_mixed, embedded)
-    grad_bias_query = jnp.sum(grad_query.astype(F32), axis=(0, 1)).reshape(mp, own_heads * HD)
-    grad_bias_value = jnp.sum(grad_value.astype(F32), axis=(0, 1)).reshape(mp, own_heads * HD)
-    grad_embed = grad_h1 + dot("tc,cd->td", grad_mixed, qkv_t)
-
+    flat = (tok_rows, heads * HD)
+    grad_query, grad_key, grad_value = grad_query.reshape(flat), grad_key.reshape(flat), grad_value.reshape(flat)
+    grad_bias_query = jnp.sum(grad_query.astype(F32), axis=0)
+    grad_bias_value = jnp.sum(grad_value.astype(F32), axis=0)
+    grad_embed = (
+        grad_h1
+        + dot("tc,cd->td", grad_query, w_query)
+        + dot("tc,cd->td", grad_key, w_key)
+        + dot("tc,cd->td", grad_value, w_value)
+    )
+    kinds = [dot("tc,td->cd", part, embedded) for part in (grad_query, grad_key, grad_value)]
     grads = jnp.stack(
         [
-            jnp.concatenate(
-                [grad_w_qkv.reshape(mp, qkv_rows, width), grad_w_out.reshape(mp, own_heads * HD, width)], axis=1
-            ),
-            grad_w_in,
-            grad_w_down,
+            jnp.stack([*kinds, grad_w_out]).reshape(mp * INNER, slice_rows, width),
+            grad_w_in.reshape(mp * INNER, slice_rows, width),
+            grad_w_down.reshape(mp * INNER, slice_rows, width),
         ]
     ).astype(BF16)
-    summed = reduce_grads(grads.reshape(BLOCKS, mp, INNER, slice_rows, width), mp)
+    vectors = [grad_gain_one, grad_shift_one, grad_bias_out, grad_gain_two, grad_shift_two, grad_bias_down]
+    vectors += [grad_bias_query, grad_bias_value, *grad_bias_in, jnp.full((width,), count_local)]
+    small = jnp.stack(vectors)
+    small = jnp.pad(small, ((0, -small.shape[0] % 8), (0, 0)))
+    outgoing = jnp.zeros((devices * capacity, width), BF16).at[slot_place].set(grad_embed.astype(BF16))
+    summed, small, incoming = reduce_grads(grads, small, outgoing.reshape(devices, capacity, width), mp)
     group = summed
     for step in range(1, dp // INNER):
         shift = [(i, (i + step * INNER) % dp) for i in range(dp)]
         summed = (summed.astype(F32) + lax.ppermute(group, "dp", shift).astype(F32)).astype(BF16)
     summed = summed.reshape(BLOCKS, shard_rows, width)
-
-    small = lax.psum(
-        (
-            count_local,
-            grad_gain_one,
-            grad_shift_one,
-            grad_bias_out,
-            grad_gain_two,
-            grad_shift_two,
-            grad_bias_down,
-            grad_bias_query,
-            grad_bias_value,
-            grad_bias_in,
-        ),
-        axes,
-    )
-    factor = lax.rsqrt(small[0])
-    gain_one_s, shift_one_s, bias_out_s, gain_two_s, shift_two_s, bias_down_s = (v * factor for v in small[1:7])
+    if dp > INNER:
+        small = jnp.sum(lax.all_gather(small, "dp")[::INNER], axis=0)
+    factor = lax.rsqrt(small[8 + mp, 0])
+    small = small * factor
+    gain_one_s, shift_one_s, bias_out_s, gain_two_s, shift_two_s, bias_down_s = (small[i] for i in range(6))
     m = lax.axis_index("mp")
-    bias_query_s, bias_value_s, bias_in_s = (v[m] * factor for v in small[7:])
-
-    outgoing = jnp.zeros((devices * capacity, width), BF16).at[slot_place].set(grad_embed.astype(BF16))
-    incoming = lax.all_to_all(
-        outgoing.reshape(devices, capacity, width), axes, split_axis=0, concat_axis=0, tiled=True
-    )
+    bias_query_s = small[6].reshape(mp, own_heads * HD)[m]
+    bias_value_s = small[7].reshape(mp, own_heads * HD)[m]
+    bias_in_s = small[8 : 8 + mp][m]
+    grad_kinds = summed[0, :qkv_rows].reshape(3, own_heads, HD, width).transpose(3, 1, 0, 2).reshape(width, qkv_rows)
     received = jnp.where(slot_live[..., None], incoming.astype(F32), F32(0.0)).reshape(devices * capacity, width)
     grad_table = jnp.zeros(table.shape, F32).at[wanted_rows.reshape(-1)].add(received * factor)
     scaled = summed.astype(F32) * factor
     return (
         activations,
         grad_table,
-        scaled[0, :qkv_rows].T,
+        grad_kinds.astype(F32) * factor,
         bias_query_s,
         bias_value_s,
         scaled[0, qkv_rows:],

time: 433 us -> 379 us (0.88)
  blocking collectives: 49.6 us -> 0 us
  Pallas kernels: 166 us -> 191 us
  starting transfers between devices: 25.6 us -> 7.08 us
  waiting for transfers between devices: 10.5 us -> 0.01 us
    psum x1 -> x0, blocking collectives: 39.1 us -> none  [on_device(): lax.psum((count_local, grad_gain_one, grad_shift_one, grad_bias_out, grad...]
    pallas_call x2, Pallas kernels: 166 us -> 191 us  [the longest x1 102 us: reduce_grads(): pl.pallas_call(partial(reduce_kernel, mp, devices), out_shape=(jax.ShapeD...]
    all_to_all x2 -> x0, starting transfers between devices: 18.5 us -> none  [the longest x1 13.5 us: on_device(): lax.all_to_all(table[wanted_rows], axes, split_axis=0, concat_axis=0, til...]
    all_to_all x2 -> x0, waiting for transfers between devices: 10.5 us -> none  [the longest x1 10.5 us: on_device(): lax.all_to_all(table[wanted_rows], axes, split_axis=0, concat_axis=0, til...]
    all_gather x1 -> x0, blocking collectives: 10.5 us -> none  [on_device(): lax.all_gather(jnp.concatenate([bias_query, bias_value, bias_in]), 'mp',...]
    slice x5 -> x6, local copies, waits for them, and re-layouts: 16.2 us -> 10.5 us  [the longest x1 8.5 us: on_device(): w_down = whole[2].reshape(mp, shard_rows, width)]
    dot_general x4 -> x9, matrix products: 10 us -> 12.4 us  [the longest x3 4.46 us: on_device(): dot('tc,td->cd', part, embedded)]
  transfers between devices with their start and end apart: 3 -> 1, of which waited for: 1 -> 0; matrix products, arithmetic and copies ran while one was open for 10% -> 4% of each run, Pallas kernels for 39% -> 0%
where the time goes in v2:
time: 379 us; the launch traced here: 372 us
  Pallas kernels  191 us (50%)
  other arithmetic  64.3 us (17%)
  local copies, waits for them, and re-layouts  61 us (16%)
  matrix products  45.2 us (12%)
  starting transfers between devices  7.08 us (2%)
    pallas_call x1, Pallas kernels, reduce_grads(): pl.pallas_call(partial(reduce_kernel, mp, devices), out_shape=(jax.ShapeD...  102 us
    pallas_call x1, Pallas kernels, gather_weights(): pl.pallas_call(partial(gather_kernel, mp, devices), out_shape=(jax.ShapeD...  88.8 us
    scatter-add x1, other arithmetic, on_device(): jnp.zeros(table.shape, F32).at[wanted_rows.reshape(-1)]  23.8 us
    gather x1, local copies, waits for them, and re-layouts, on_device(): table[wanted_rows]  14 us
    slice x1, local copies, waits for them, and re-layouts, on_device(): w_down = whole[2].reshape(mp, shard_rows, width)  8.5 us
    convert_element_type x1, other arithmetic, on_device(): hidden_act = gelu_val.astype(BF16)  7.65 us
  transfers between devices with their start and end apart: 1, of which 0 were waited for; matrix products, arithmetic and copies ran while one was open for 4% of the time, Pallas kernels for 0%

profile of v2, /device:TPU:1, one launch (start us, length us, event | category | flops | bytes accessed | tf_op | source)
XLA Modules:
  0.0 372.2 jit_solution(7236667968030739120)
XLA Ops:
  6.0 7.1 %all-to-all-start = ((s32[32,1,16]{2,1,0:T(1,128)}), s32[32,1,16]{2,1,0:T(1,128)S(1)}, u32[]{:S(2)}, u32[]{:S(2)}) async-start(s32[32,1,16]{2,1,0:T(1,128)} %bitcast.12), calls=%async_computation | async-start | bytes 32768 | tf_op jit(solution)/shard_map/all_to_all | solution.py:516
  20.1 2.0 pad_maximum_fusion.2.own_ref
  29.1 14.0 %gather_fusion = bf16[512,768]{1,0:T(8,128)(2,1)} fusion(bf16[15664,768]{1,0:T(8,128)(2,1)} %param.23, s32[1024]{0:T(1024)S(1)} %pad_clamp_fusion.1), kind=kCustom, calls=%fused_computation | custom fusion | bytes 1574912 | tf_op jit(solution)/shard_map/gather | solution.py:520
  43.2 88.8 %shard_map.298 = (bf16[3,32,96,768]{3,2,1,0:T(8,128)(2,1)}, bf16[4,16,128]{2,1,0:T(8,128)(2,1)}, bf16[32,16,768]{2,1,0:T(8,128)(2,1)}) custom-call(bf16[3,8,96,768]{3,2,1,0:T(8,128)(2,1)} %pad_maximum_fusion.2.own_ref, bf16[16,128]{1,0:T(8,128)(2,1)} %pad.8.bias_ref, bf16[32,16,768]{2,1,0:T(8,128)(2,1)} %bitcast.199), custom_call_target="tpu_custom_call" | custom-call | tf_op jit(solution)/shard_map/pallas_call | solution.py:246
  132.8 4.0 %fusion.56 = (bf16[1,8,96,768]{3,2,1,0:T(8,128)(2,1)S(1)}, bf16[1,8,96,768]{3,2,1,0:T(8,128)(2,1)S(1)}, bf16[1,8,96,768]{3,2,1,0:T(8,128)(2,1)}, bf16[1,8,96,768]{3,2,1,0:T(8,128)(2,1)}) fusion(bf16[3,32,96,768]{3,2,1,0:T(8,128)(2,1)} %get-tuple-element.22), kind=kLoop, calls=%fused_computation.163 | loop fusion | bytes 9437184 | tf_op jit(solution)/shard_map/unstack | solution.py:523
  136.9 8.5 %fusion.55 = (bf16[1,32,96,768]{3,2,1,0:T(8,128)(2,1)}, bf16[1,32,96,768]{3,2,1,0:T(8,128)(2,1)}) fusion(bf16[3,32,96,768]{3,2,1,0:T(8,128)(2,1)} %get-tuple-element.22), kind=kLoop, calls=%fused_computation.162 | loop fusion | bytes 18874368 | tf_op jit(solution)/shard_map/slice | solution.py:525
  153.2 2.0 fusion.57
  160.6 4.6 %fusion.28 = (u8[256,768]{1,0:T(8,128)(4,1)S(1)}, u8[256,768]{1,0:T(8,128)(4,1)S(1)}, f32[256,4,768]{2,0,1:T(8,128)S(1)}) fusion(f32[4,768]{1,0:T(4,128)S(1)} %slice_convert_fusion, bf16[4,768,768]{2,1,0:T(8,128)(2,1)} %bitcast.189, f32[256,768]{1,0:T(8,128)S(1)} %get-tuple-element.65, f32[768]{0:T(1024)S(1)} %copy-done.34, ...), kind=kOutput, calls=%fused_computation.95 | convolution fusion | flops 1219559424 | bytes 9064448 | tf_op jit(solution)/shard_map/td,mdf->tmf/dot_general | solution.py:563
  165.3 7.7 %multiply_convert_fusion = (bf16[256,4,768]{2,0,1:T(8,128)(2,1)S(1)}, f32[256,4,768]{2,0,1:T(8,128)S(1)}) fusion(f32[256,4,768]{2,0,1:T(8,128)S(1)} %get-tuple-element.66, f32[4,768]{1,0:T(4,128)S(1)} %slice_convert_fusion, u8[256,768]{1,0:T(8,128)(4,1)S(1)} %get-tuple-element.28, u8[256,768]{1,0:T(8,128)(4,1)S(1)} %get-tuple-element.27), kind=kLoop, calls=%fused_computation.21 | loop fusion | flops 55836672 | bytes 8269824 | tf_op jit(solution)/shard_map/convert_element_type | solution.py:565
  175.9 1.7 fusion.52
  177.6 2.8 convert_reduce_fusion
  180.5 2.2 multiply_reduce_fusion.2
  185.8 1.8 reshape.369
  187.6 3.5 convert_reduce_fusion.1
  195.5 3.8 %convolution_convert_fusion.1 = bf16[4,768,768]{1,2,0:T(8,128)(2,1)} fusion(bf16[256,4,768]{2,0,1:T(8,128)(2,1)S(1)} %copy-done.18, f32[256,768]{1,0:T(8,128)S(1)} %get-tuple-element.65, f32[768]{0:T(1024)S(1)} %copy-done.35, f32[768]{0:T(1024)S(1)} %convert_element_type.163, f32[256]{0:T(256)S(1)} %copy-done.44, f32[256]{0:T(256)S(1)} %copy-done.30), kind=kOutput, calls=%fused_computation.35 | convolution fusion | flops 1211301888 | bytes 7086080 | tf_op jit(solution)/shard_map/td,tmf->mdf/dot_general | solution.py:579
  199.3 3.6 convolution_convert_fusion
  212.6 1.9 convolution_add_fusion.2
  218.6 2.7 scatter_custom_fusion.1
  222.1 2.6 pad_maximum_fusion.1
  224.7 6.9 %pad_maximum_fusion.grad_ref = bf16[3,32,96,768]{3,2,1,0:T(8,128)(2,1)} fusion(bf16[1,32,96,768]{3,2,1,0:T(8,128)(2,1)} %bitcast.172, bf16[1,32,96,768]{3,2,1,0:T(8,128)(2,1)S(1)} %bitcast.171, bf16[1,32,96,768]{3,2,1,0:T(8,128)(2,1)S(1)} %bitcast.173), kind=kLoop, calls=%fused_computation.8 | loop fusion | flops 14155776 | bytes 28311552 | tf_op jit(solution)/shard_map/stack | solution.py:602
  231.6 102.3 %shard_map.299 = (bf16[3,8,96,768]{3,2,1,0:T(8,128)(2,1)}, f32[16,768]{1,0:T(8,128)}, bf16[32,16,768]{2,1,0:T(8,128)(2,1)}) custom-call(bf16[3,32,96,768]{3,2,1,0:T(8,128)(2,1)} %pad_maximum_fusion.grad_ref, f32[16,768]{1,0:T(8,128)} %pad.9.small_ref, bf16[32,16,768]{2,1,0:T(8,128)(2,1)} %bitcast.198), custom_call_target="tpu_custom_call" | custom-call | tf_op jit(solution)/shard_map/pallas_call | solution.py:422
  337.2 2.6 convert_multiply_fusion
  340.7 2.5 slice_bitcast_fusion
  348.0 23.8 %scatter_custom_fusion.2 = f32[15664,768]{1,0:T(8,128)} fusion(s32[512]{0:T(512)} %copy-done.46, f32[512,768]{1,0:T(8,128)S(1)} %bitcast.201, f32[]{:T(128)} %constant.55.clone.1), kind=kCustom, calls=%fused_computation.6 | custom fusion | flops 393216 | bytes 48120320 | tf_op jit(solution)/shard_map/scatter-add | solution.py:631
  (255 shorter events, 65.4 us)
Async XLA Ops:
  0.6 19.3 %copy-start.20 = (bf16[768,768]{1,0:T(8,128)(2,1)S(1)}, bf16[768,768]{1,0:T(8,128)(2,1)}, u32[]{:S(2)}) copy-start(bf16[768,768]{1,0:T(8,128)(2,1)} %param.33) | copy-start | bytes 3538948
  0.7 19.3 %copy-start.21 = (bf16[768,768]{1,0:T(8,128)(2,1)S(1)}, bf16[768,768]{1,0:T(8,128)(2,1)}, u32[]{:S(2)}) copy-start(bf16[768,768]{1,0:T(8,128)(2,1)} %param.31) | copy-start | bytes 3538948
  3.8 18.3 %copy-start.51 = (s32[256,1]{0,1:T(1,128)}, s32[256,1]{0,1:T(1,128)S(1)}, u32[]{:S(2)}) copy-start(s32[256,1]{0,1:T(1,128)S(1)} %compare_select_fusion) | copy-start | bytes 3076
  6.0 22.3 %all-to-all-start = ((s32[32,1,16]{2,1,0:T(1,128)}), s32[32,1,16]{2,1,0:T(1,128)S(1)}, u32[]{:S(2)}, u32[]{:S(2)}) async-start(s32[32,1,16]{2,1,0:T(1,128)} %bitcast.12), calls=%async_computation | async-start | bytes 32768 | tf_op jit(solution)/shard_map/all_to_all | solution.py:516
  20.0 5.2 %copy-start.58 = (bf16[768]{0:T(1024)(128)(2,1)S(1)}, bf16[768]{0:T(1024)(128)(2,1)}, u32[]{:S(2)}) copy-start(bf16[768]{0:T(1024)(128)(2,1)} %param.28) | copy-start | bytes 4612
  20.0 5.8 %copy-start.59 = (bf16[768]{0:T(1024)(128)(2,1)S(1)}, bf16[768]{0:T(1024)(128)(2,1)}, u32[]{:S(2)}) copy-start(bf16[768]{0:T(1024)(128)(2,1)} %param.34) | copy-start | bytes 4612
  20.0 6.4 %copy-start.60 = (bf16[768]{0:T(1024)(128)(2,1)S(1)}, bf16[768]{0:T(1024)(128)(2,1)}, u32[]{:S(2)}) copy-start(bf16[768]{0:T(1024)(128)(2,1)} %param.36) | copy-start | bytes 4612
  20.0 7.6 %copy-start.61 = (bf16[768]{0:T(1024)(128)(2,1)S(1)}, bf16[768]{0:T(1024)(128)(2,1)}, u32[]{:S(2)}) copy-start(bf16[768]{0:T(1024)(128)(2,1)} %param.32) | copy-start | bytes 4612
  20.0 7.6 %copy-start.62 = (bf16[192]{0:T(256)(128)(2,1)S(1)}, bf16[192]{0:T(256)(128)(2,1)}, u32[]{:S(2)}) copy-start(bf16[192]{0:T(256)(128)(2,1)} %param.25) | copy-start | bytes 1156
  20.0 7.6 %copy-start.63 = (bf16[192]{0:T(256)(128)(2,1)S(1)}, bf16[192]{0:T(256)(128)(2,1)}, u32[]{:S(2)}) copy-start(bf16[192]{0:T(256)(128)(2,1)} %param.26) | copy-start | bytes 1156
  29.1 14.0 %copy-start.46 = (s32[512]{0:T(512)}, s32[512]{0:T(512)S(1)}, u32[]{:S(2)}) copy-start(s32[512]{0:T(512)S(1)} %reshape.319) | copy-start | bytes 6148
  136.9 11.2 %copy-start.3 = (bf16[1,8,96,768]{3,2,1,0:T(8,128)(2,1)}, bf16[1,8,96,768]{3,2,1,0:T(8,128)(2,1)S(1)}, u32[]{:S(2)}) copy-start(bf16[1,8,96,768]{3,2,1,0:T(8,128)(2,1)S(1)} %get-tuple-element.54) | copy-start | bytes 3538948
  136.9 9.8 %copy-start = (bf16[32,16,768]{2,1,0:T(8,128)(2,1)S(1)}, bf16[32,16,768]{2,1,0:T(8,128)(2,1)}, u32[]{:S(2)}) copy-start(bf16[32,16,768]{2,1,0:T(8,128)(2,1)} %get-tuple-element.21) | copy-start | bytes 2359300
  160.4 22.3 %copy-start.29 = (f32[256]{0:T(256)}, f32[256]{0:T(256)S(1)}, u32[]{:S(2)}) copy-start(f32[256]{0:T(256)S(1)} %broadcast_multiply_fusion.6) | copy-start | bytes 3076
  160.4 12.6 %slice-start.4 = ((s8[4718592]{0:T(1024)(128)(4,1)}), s8[4194304]{0:T(1024)(128)(4,1)S(1)}, s32[]{:S(2)}) async-start(s8[4718592]{0:T(1024)(128)(4,1)} %bitcast.193), calls=%async_computation.5 | async-start | bytes 8388608
  160.6 22.1 %copy-start.43 = (f32[256]{0:T(256)}, f32[256]{0:T(256)S(1)}, u32[]{:S(2)}) copy-start(f32[256]{0:T(256)S(1)} %add_rsqrt_fusion.1) | copy-start | bytes 3076
  160.6 12.3 %slice-start.5 = ((s8[4718592]{0:T(1024)(128)(4,1)}), s8[524288]{0:T(1024)(128)(4,1)S(1)}, s32[]{:S(2)}) async-start(s8[4718592]{0:T(1024)(128)(4,1)} %bitcast.193), calls=%async_computation.6 | async-start | bytes 1048576
  165.3 7.7 %copy-start.54 = (f32[768]{0:T(1024)S(1)}, f32[768]{0:T(1024)}, u32[]{:S(2)}) copy-start(f32[768]{0:T(1024)} %convert_element_type.168) | copy-start | bytes 9220
  199.3 4.8 %copy-start.52 = (f32[768]{0:T(1024)S(1)}, f32[768]{0:T(1024)}, u32[]{:S(2)}) copy-start(f32[768]{0:T(1024)} %get-tuple-element.34) | copy-start | bytes 9220
  199.3 8.1 %copy-start.50 = (f32[12,64]{1,0:T(8,128)S(1)}, f32[12,64]{1,0:T(8,128)}, u32[]{:S(2)}) copy-start(f32[12,64]{1,0:T(8,128)} %get-tuple-element.74) | copy-start | bytes 9220
  202.9 7.2 %copy-start.14 = (bf16[4,64,12,64]{3,1,2,0:T(8,128)(2,1)S(1)}, bf16[4,64,12,64]{3,1,2,0:T(8,128)(2,1)}, u32[]{:S(2)}) copy-start(bf16[4,64,12,64]{3,1,2,0:T(8,128)(2,1)} %get-tuple-element.73) | copy-start | bytes 1179652
  212.6 4.9 %copy-start.4 = (bf16[1,8,96,768]{3,2,1,0:T(8,128)(2,1)S(1)}, bf16[1,8,96,768]{3,2,1,0:T(8,128)(2,1)}, u32[]{:S(2)}) copy-start(bf16[1,8,96,768]{3,2,1,0:T(8,128)(2,1)} %copy-done.3) | copy-start | bytes 3538948
  217.5 4.6 %copy-start.6 = (bf16[1,768,768]{2,1,0:T(8,128)(2,1)S(1)}, bf16[1,768,768]{2,1,0:T(8,128)(2,1)}, u32[]{:S(2)}) copy-start(bf16[1,768,768]{2,1,0:T(8,128)(2,1)} %fusion.14) | copy-start | bytes 3538948
  343.1 4.6 %copy-start.24 = (bf16[32,16,768]{2,1,0:T(8,128)(2,1)S(1)}, bf16[32,16,768]{2,1,0:T(8,128)(2,1)}, u32[]{:S(2)}) copy-start(bf16[32,16,768]{2,1,0:T(8,128)(2,1)} %get-tuple-element.24) | copy-start | bytes 2359300
  (51 other events, 148.4 us)

commit v3 on v2

--- a/solution.py
+++ b/solution.py
@@ -449,21 +449,247 @@
     )(grads, small, rows)
 
 
+NN = (((1,), (0,)), ((), ()))
+NT = (((1,), (1,)), ((), ()))
+TN = (((0,), (0,)), ((), ()))
+ROOT_HALF = 0.7071067811865476
+DENSITY = 0.3989422804014327
+
+
+def mul(lhs, rhs, dims):
+    return lax.dot_general(lhs, rhs, dims, preferred_element_type=F32)
+
+
+def row_mean(v):
+    return jnp.mean(v, axis=1, keepdims=True)
+
+
+def column_sum(v):
+    return jnp.sum(v, axis=0, keepdims=True)
+
+
 def norm_rows(hidden, gain_vec, shift_vec):
-    row_mean = jnp.mean(hidden, axis=-1, keepdims=True)
-    centred = hidden - row_mean
-    variance = jnp.mean(centred * centred, axis=-1, keepdims=True)
-    row_scale = lax.rsqrt(variance + EPS)
+    centred = hidden - row_mean(hidden)
+    row_scale = lax.rsqrt(row_mean(centred * centred) + EPS)
     normed = centred * row_scale
-    return (normed * gain_vec + shift_vec, normed, row_scale)
+    return normed * gain_vec + shift_vec, normed, row_scale
 
 
 def norm_back(grad_out, normed, row_scale, gain_vec):
     grad_normed = grad_out * gain_vec
-    inner_mean = jnp.mean(grad_normed, axis=-1, keepdims=True)
-    cross_mean = jnp.mean(grad_normed * normed, axis=-1, keepdims=True)
-    grad_in = row_scale * (grad_normed - inner_mean - normed * cross_mean)
-    return (grad_in, jnp.sum(grad_out * normed, axis=0), jnp.sum(grad_out, axis=0))
+    return row_scale * (grad_normed - row_mean(grad_normed) - normed * row_mean(grad_normed * normed))
+
+
+def layer_kernel(
+    mp,
+    slot_col,
+    slot_row,
+    weight_col,
+    live_col,
+    rows_ref,
+    w_ref,
+    bias_ref,
+    bias_in_ref,
+    vec_ref,
+    cot_ref,
+    count_ref,
+    act_out,
+    grad_ref,
+    small_ref,
+    rows_out,
+    emb,
+    qkv,
+    probs,
+    ctx,
+    first,
+    normed,
+    first_low,
+    acc,
+    act,
+    slope,
+    grad_low,
+    grad_qkv,
+    acc_two,
+):
+    tokens, width = act_out.shape
+    slots = rows_ref.shape[0]
+    per_kind = 2 * mp
+    pairs = width // 128
+
+    def weight(a, at, number):
+        return w_ref[a, pl.ds(at, number)].reshape(width, width)
+
+    def put(a, at, number, value):
+        grad_ref[a, pl.ds(at, number)] = value.astype(BF16).reshape(number, width // number, width)
+
+    def vec(i):
+        return vec_ref[i : i + 1, :]
+
+    pick = (lax.broadcasted_iota(jnp.int32, (tokens, slots), 1) == slot_col[...]).astype(F32).astype(BF16)
+    emb[...] = mul(pick, rows_ref[...], NN).astype(BF16)
+
+    def project(j, _):
+        qkv[j] = (mul(emb[...], weight(0, j * per_kind, per_kind), NT) + bias_ref[j]).astype(BF16)
+        return 0
+
+    lax.fori_loop(0, 3, project, 0)
+
+    low_half = lax.broadcasted_iota(jnp.int32, (1, 128), 1) < HD
+
+    def halves(v):
+        zero = jnp.zeros_like(v)
+        return jnp.where(low_half, v, zero), jnp.where(low_half, zero, v)
+
+    def lanes(pair):
+        return pl.ds(pl.multiple_of(pair * 128, 128), 128)
+
+    def attend(pair, _):
+        key_sent = lax.div(lax.broadcasted_iota(jnp.int32, (tokens, tokens), 0), SEQ)
+        query_sent = lax.div(lax.broadcasted_iota(jnp.int32, (tokens, tokens), 1), SEQ)
+        seen = jnp.logical_and(key_sent == query_sent, live_col[...] > 0.0)
+        keys = qkv[1, :, lanes(pair)]
+        values = qkv[2, :, lanes(pair)]
+        parts = []
+        for half, queries in enumerate(halves(qkv[0, :, lanes(pair)])):
+            scores = jnp.where(seen, mul(keys, queries, NT) * 0.125, F32(-1e30))
+            weights = jnp.exp(scores - jnp.max(scores, axis=0, keepdims=True))
+            weights = weights / column_sum(weights)
+            probs[2 * pair + half] = weights
+            parts.append(mul(weights.astype(BF16), values, TN))
+        ctx[:, lanes(pair)] = jnp.where(low_half, parts[0], parts[1]).astype(BF16)
+        return 0
+
+    lax.fori_loop(0, pairs, attend, 0)
+
+    hidden = emb[...].astype(F32) + mul(ctx[...], weight(0, 3 * per_kind, per_kind), NN) + vec(2)
+    first_value, normed_one, scale_one = norm_rows(hidden, vec(0), vec(1))
+    first[...] = first_value
+    normed[...] = normed_one
+    first_low[...] = first_value.astype(BF16)
+    acc[...] = first_value + vec(5)
+
+    def feed(m, _):
+        pre = mul(first_low[...], weight(1, m * INNER, INNER), NN) + bias_in_ref[m]
+        half_gate = 0.5 + 0.5 * lax.erf(pre * ROOT_HALF)
+        act[m] = (pre * half_gate).astype(BF16)
+        slope[m] = half_gate + pre * (jnp.exp(-0.5 * pre * pre) * DENSITY)
+        acc[...] += mul(act[m], weight(2, m * INNER, INNER), NN)
+        return 0
+
+    lax.fori_loop(0, mp, feed, 0)
+
+    final, normed_two, scale_two = norm_rows(acc[...], vec(3), vec(4))
+    act_out[...] = final.astype(BF16)
+    grad_final = weight_col[...] * cot_ref[...].astype(F32)
+    small_ref[3:4, :] = column_sum(grad_final * normed_two)
+    small_ref[4:5, :] = column_sum(grad_final)
+    grad_h2 = norm_back(grad_final, normed_two, scale_two, vec(3))
+    small_ref[5:6, :] = column_sum(grad_h2)
+    grad_low[...] = grad_h2.astype(BF16)
+    acc[...] = grad_h2
+
+    def feed_back(m, _):
+        put(2, m * INNER, INNER, mul(act[m], grad_low[...], TN))
+        grad_pre = mul(grad_low[...], weight(2, m * INNER, INNER), NT) * slope[m]
+        low = grad_pre.astype(BF16)
+        small_ref[pl.ds(8 + m, 1), :] = column_sum(low.astype(F32))
+        put(1, m * INNER, INNER, mul(first_low[...], low, TN))
+        acc[...] += mul(low, weight(1, m * INNER, INNER), NT)
+        return 0
+
+    lax.fori_loop(0, mp, feed_back, 0)
+
+    grad_first = acc[...]
+    small_ref[0:1, :] = column_sum(grad_first * normed[...])
+    small_ref[1:2, :] = column_sum(grad_first)
+    grad_h1 = norm_back(grad_first, normed[...], scale_one, vec(0))
+    small_ref[2:3, :] = column_sum(grad_h1)
+    acc_two[...] = grad_h1
+    grad_attn = grad_h1.astype(BF16)
+    put(0, 3 * per_kind, per_kind, mul(ctx[...], grad_attn, TN))
+    grad_low[...] = mul(grad_attn, weight(0, 3 * per_kind, per_kind), NT).astype(BF16)
+
+    def attend_back(pair, _):
+        queries = qkv[0, :, lanes(pair)]
+        keys = qkv[1, :, lanes(pair)]
+        values = qkv[2, :, lanes(pair)]
+        grad_ctx = grad_low[:, lanes(pair)]
+        parts = []
+        for half, masked in enumerate(halves(grad_ctx)):
+            weights = probs[2 * pair + half]
+            grad_probs = mul(values, masked, NT)
+            grad_scores = weights * (grad_probs - column_sum(grad_probs * weights))
+            grad_scores = grad_scores.astype(BF16)
+            parts.append(
+                (
+                    mul(grad_scores, keys, TN) * 0.125,
+                    mul(grad_scores, queries, NN) * 0.125,
+                    mul(weights.astype(BF16), grad_ctx, NN),
+                )
+            )
+        for j in range(3):
+            grad_qkv[j, :, lanes(pair)] = jnp.where(low_half, parts[0][j], parts[1][j]).astype(BF16)
+        return 0
+
+    lax.fori_loop(0, pairs, attend_back, 0)
+
+    def project_back(j, _):
+        put(0, j * per_kind, per_kind, mul(grad_qkv[j], emb[...], TN))
+        acc_two[...] += mul(grad_qkv[j], weight(0, j * per_kind, per_kind), NN)
+        return 0
+
+    lax.fori_loop(0, 3, project_back, 0)
+    small_ref[6:7, :] = column_sum(grad_qkv[0].astype(F32))
+    small_ref[7:8, :] = column_sum(grad_qkv[2].astype(F32))
+    small_ref[8 + mp :, :] = jnp.broadcast_to(count_ref[...], (small_ref.shape[0] - 8 - mp, width))
+    unpick = (lax.broadcasted_iota(jnp.int32, (slots, tokens), 0) == slot_row[...]).astype(F32).astype(BF16)
+    rows_out[...] = mul(unpick, acc_two[...].astype(BF16), NN).astype(BF16)
+
+
+def layer(mp, slot_place, row_weight, token_live, rows, whole, bias_qkv, bias_in, vectors, cotangent, count):
+    tokens, width = cotangent.shape
+    heads = width // HD
+    vmem = pl.BlockSpec(memory_space=pltpu.VMEM)
+    small_rows = -(-(9 + mp) // 8) * 8
+    return pl.pallas_call(
+        partial(layer_kernel, mp),
+        out_shape=(
+            jax.ShapeDtypeStruct((tokens, width), BF16),
+            jax.ShapeDtypeStruct(whole.shape, BF16),
+            jax.ShapeDtypeStruct((small_rows, width), F32),
+            jax.ShapeDtypeStruct(rows.shape, BF16),
+        ),
+        in_specs=[vmem] * 11,
+        out_specs=(vmem,) * 4,
+        scratch_shapes=[
+            pltpu.VMEM((tokens, width), BF16),
+            pltpu.VMEM((3, tokens, width), BF16),
+            pltpu.VMEM((heads, tokens, tokens), F32),
+            pltpu.VMEM((tokens, width), BF16),
+            pltpu.VMEM((tokens, width), F32),
+            pltpu.VMEM((tokens, width), F32),
+            pltpu.VMEM((tokens, width), BF16),
+            pltpu.VMEM((tokens, width), F32),
+            pltpu.VMEM((mp, tokens, width), BF16),
+            pltpu.VMEM((mp, tokens, width), F32),
+            pltpu.VMEM((tokens, width), BF16),
+            pltpu.VMEM((3, tokens, width), BF16),
+            pltpu.VMEM((tokens, width), F32),
+        ],
+        compiler_params=pltpu.CompilerParams(vmem_limit_bytes=62 * 1024 * 1024),
+    )(
+        slot_place.reshape(tokens, 1),
+        slot_place.reshape(1, tokens),
+        row_weight.reshape(tokens, 1),
+        token_live.reshape(tokens, 1),
+        rows,
+        whole,
+        bias_qkv,
+        bias_in,
+        vectors,
+        cotangent,
+        count,
+    )
 
 
 def on_device(
@@ -498,7 +724,6 @@
     shard_rows = weight_down.shape[0]
     qkv_rows = weight_qkv.shape[1]
     own_heads = qkv_rows // (3 * HD)
-    heads = own_heads * mp
     slice_rows = shard_rows // INNER
 
     kinds = weight_qkv.reshape(width, own_heads, 3, HD).transpose(2, 1, 3, 0).reshape(qkv_rows, width)
@@ -519,14 +744,11 @@
     whole, bias_all, fetched = gather_weights(
         own.reshape(BLOCKS, INNER, slice_rows, width), bias_own, table[wanted_rows], mp
     )
-    embedded = fetched.reshape(devices * capacity, width)[slot_place]
-    w_query, w_key, w_value, w_out = whole[0].reshape(4, heads * HD, width)
-    w_in = whole[1].reshape(mp, shard_rows, width)
-    w_down = whole[2].reshape(mp, shard_rows, width)
-    bias_all = bias_all.reshape(mp, -1)
-    b_query = bias_all[:, : own_heads * HD].reshape(heads, HD).astype(F32)
-    b_value = bias_all[:, own_heads * HD : 2 * own_heads * HD].reshape(heads, HD).astype(F32)
-    b_in = bias_all[:, 2 * own_heads * HD : 2 * own_heads * HD + bias_in.shape[0]].astype(F32)
+    bias_all = bias_all.reshape(mp, -1).astype(F32)
+    b_query = bias_all[:, : own_heads * HD].reshape(1, width)
+    b_value = bias_all[:, own_heads * HD : 2 * own_heads * HD].reshape(1, width)
+    b_in = bias_all[:, 2 * own_heads * HD : 2 * own_heads * HD + bias_in.shape[0]].reshape(mp, 1, width)
+    bias_qkv = jnp.stack([b_query, jnp.zeros_like(b_query), b_value])
 
     total_sent = sent_local * devices
     group_num = group_counts.shape[0]
@@ -540,77 +762,20 @@
     row_weight = (token_live * sent_weight[:, None]).reshape(tok_rows)
     count_local = jnp.sum(lengths).astype(F32)
 
-    dot = partial(jnp.einsum, preferred_element_type=F32)
-    by_head = (sent_local, SEQ, heads, HD)
-    queries = (dot("td,cd->tc", embedded, w_query).reshape(by_head) + b_query).astype(BF16)
-    key_rows = dot("td,cd->tc", embedded, w_key).reshape(by_head).astype(BF16)
-    value_rows = (dot("td,cd->tc", embedded, w_value).reshape(by_head) + b_value).astype(BF16)
-    scores = dot("sqhe,skhe->shqk", queries, key_rows) * 0.125
-    valid = positions[None, :] < lengths[:, None]
-    scores = jnp.where(valid[:, None, None, :], scores, F32(-1e30))
-    probs = jax.nn.softmax(scores, axis=-1)
-    probs_low = probs.astype(BF16)
-    context = dot("shqk,skhe->sqhe", probs_low, value_rows).astype(BF16)
-    context_rows = context.reshape(tok_rows, heads * HD)
-    gain_one_f = gain_one.astype(F32)
-    gain_two_f = gain_two.astype(F32)
-    first_out, normed_one, scale_one = norm_rows(
-        embedded.astype(F32) + dot("tc,cd->td", context_rows, w_out) + bias_out.astype(F32),
-        gain_one_f,
-        shift_one.astype(F32),
+    vectors = jnp.stack([gain_one, shift_one, bias_out, gain_two, shift_two, bias_down]).astype(F32)
+    activations, grads, small, outgoing = layer(
+        mp,
+        slot_place,
+        row_weight,
+        token_live,
+        fetched.reshape(devices * capacity, width),
+        whole,
+        bias_qkv,
+        b_in,
+        vectors,
+        cotangent,
+        count_local.reshape(1, 1),
     )
-    first_low = first_out.astype(BF16)
-    hidden_pre = dot("td,mdf->tmf", first_low, w_in) + b_in
-    gelu_val, gelu_pull = jax.vjp(partial(jax.nn.gelu, approximate=False), hidden_pre)
-    hidden_act = gelu_val.astype(BF16)
-    down_sum = dot("tmf,mfd->td", hidden_act, w_down)
-    final_out, normed_two, scale_two = norm_rows(
-        first_out + down_sum + bias_down.astype(F32), gain_two_f, shift_two.astype(F32)
-    )
-    activations = final_out.astype(BF16)
-    grad_final = row_weight[:, None] * cotangent.astype(F32)
-    grad_h2, grad_gain_two, grad_shift_two = norm_back(grad_final, normed_two, scale_two, gain_two_f)
-    grad_bias_down = jnp.sum(grad_h2, axis=0)
-    grad_down = grad_h2.astype(BF16)
-    grad_w_down = dot("tmf,td->mfd", hidden_act, grad_down)
-    grad_act = dot("td,mfd->tmf", grad_down, w_down)
-    grad_pre = gelu_pull(grad_act)[0].astype(BF16)
-    grad_bias_in = jnp.sum(grad_pre.astype(F32), axis=0)
-    grad_w_in = dot("td,tmf->mdf", first_low, grad_pre)
-    grad_first = grad_h2 + dot("tmf,mdf->td", grad_pre, w_in)
-    grad_h1, grad_gain_one, grad_shift_one = norm_back(grad_first, normed_one, scale_one, gain_one_f)
-    grad_bias_out = jnp.sum(grad_h1, axis=0)
-    grad_attn = grad_h1.astype(BF16)
-    grad_w_out = dot("tc,td->cd", context_rows, grad_attn)
-    grad_context = dot("td,cd->tc", grad_attn, w_out).astype(BF16).reshape(sent_local, SEQ, heads, HD)
-    grad_probs = dot("sqhe,skhe->shqk", grad_context, value_rows)
-    grad_value = dot("shqk,sqhe->skhe", probs_low, grad_context).astype(BF16)
-    grad_scores = (probs * (grad_probs - jnp.sum(grad_probs * probs, axis=-1, keepdims=True))).astype(BF16)
-    grad_query = (dot("shqk,skhe->sqhe", grad_scores, key_rows) * 0.125).astype(BF16)
-    grad_key = (dot("shqk,sqhe->skhe", grad_scores, queries) * 0.125).astype(BF16)
-    flat = (tok_rows, heads * HD)
-    grad_query, grad_key, grad_value = grad_query.reshape(flat), grad_key.reshape(flat), grad_value.reshape(flat)
-    grad_bias_query = jnp.sum(grad_query.astype(F32), axis=0)
-    grad_bias_value = jnp.sum(grad_value.astype(F32), axis=0)
-    grad_embed = (
-        grad_h1
-        + dot("tc,cd->td", grad_query, w_query)
-        + dot("tc,cd->td", grad_key, w_key)
-        + dot("tc,cd->td", grad_value, w_value)
-    )
-    kinds = [dot("tc,td->cd", part, embedded) for part in (grad_query, grad_key, grad_value)]
-    grads = jnp.stack(
-        [
-            jnp.stack([*kinds, grad_w_out]).reshape(mp * INNER, slice_rows, width),
-            grad_w_in.reshape(mp * INNER, slice_rows, width),
-            grad_w_down.reshape(mp * INNER, slice_rows, width),
-        ]
-    ).astype(BF16)
-    vectors = [grad_gain_one, grad_shift_one, grad_bias_out, grad_gain_two, grad_shift_two, grad_bias_down]
-    vectors += [grad_bias_query, grad_bias_value, *grad_bias_in, jnp.full((width,), count_local)]
-    small = jnp.stack(vectors)
-    small = jnp.pad(small, ((0, -small.shape[0] % 8), (0, 0)))
-    outgoing = jnp.zeros((devices * capacity, width), BF16).at[slot_place].set(grad_embed.astype(BF16))
     summed, small, incoming = reduce_grads(grads, small, outgoing.reshape(devices, capacity, width), mp)
     group = summed
     for step in range(1, dp // INNER):

time: 379 us -> 310 us (0.82); the launches traced: 372 us -> 309 us
  matrix products: 45.2 us -> 0 us
  Pallas kernels: 191 us -> 230 us
  local copies, waits for them, and re-layouts: 61 us -> 31.1 us
  other arithmetic: 64.3 us -> 38.3 us
    dot_general x23 -> x0, matrix products: 43.2 us -> none  [the longest x1 4.61 us: on_device(): hidden_pre = dot('td,mdf->tmf', first_low, w_in) + b_in]
    pallas_call x0 -> x1, Pallas kernels: none -> 39.3 us  [layer(): pl.pallas_call(partial(layer_kernel, mp), out_shape=(jax.ShapeDtypeStruct...]
    convert_element_type x10 -> x2, other arithmetic: 11.2 us -> 0.68 us  [the longest x1 0.61 us: on_device(): jnp.stack([gain_one, shift_one, bias_out, gain_two, shift_two, bias_down])]
    another operation x6 -> x5, other arithmetic: 10.3 us -> 1.53 us  [the longest x1 6.85 us: on_device(): jnp.stack([jnp.stack([*kinds, grad_w_out]).reshape(mp * INNER, slice_rows...]
    slice x2 -> x3, local copies, waits for them, and re-layouts: 8.68 us -> 0.26 us  [the longest x1 8.5 us: on_device(): w_down = whole[2].reshape(mp, shard_rows, width)]
    another operation x13 -> x12, local copies, waits for them, and re-layouts: 7.97 us -> 1.09 us  [the longest x1 4.05 us: on_device(): w_query, w_key, w_value, w_out = whole[0].reshape(4, heads * HD, width)]
    convert_element_type x6 -> x1, local copies, waits for them, and re-layouts: 5.6 us -> 0.79 us  [on_device(): token_live = (positions[None, :] < lengths[:, None]).astype(F32)]
  transfers between devices with their start and end apart: 1 -> 1, of which waited for: 0 -> 0; matrix products, arithmetic and copies ran while one was open for 4% -> 3% of each run, Pallas kernels for 0% -> 0%
where the time goes in v3:
time: 310 us; the launch traced here: 309 us
  Pallas kernels  230 us (74%)
  other arithmetic  38.3 us (12%)
  local copies, waits for them, and re-layouts  31.1 us (10%)
  starting transfers between devices  7.08 us (2%)
    pallas_call x1, Pallas kernels, reduce_grads(): pl.pallas_call(partial(reduce_kernel, mp, devices), out_shape=(jax.ShapeD...  102 us
    pallas_call x1, Pallas kernels, gather_weights(): pl.pallas_call(partial(gather_kernel, mp, devices), out_shape=(jax.ShapeD...  88.6 us
    pallas_call x1, Pallas kernels, layer(): pl.pallas_call(partial(layer_kernel, mp), out_shape=(jax.ShapeDtypeStruct...  39.3 us
    scatter-add x1, other arithmetic, on_device(): jnp.zeros(table.shape, F32).at[wanted_rows.reshape(-1)]  23.4 us
    gather x1, local copies, waits for them, and re-layouts, on_device(): table[wanted_rows]  14 us
    all_to_all x1, starting transfers between devices, on_device(): lax.all_to_all(requests.reshape(devices, capacity), axes, split_axis=0, c...  7.08 us
  transfers between devices with their start and end apart: 1, of which 0 were waited for; matrix products, arithmetic and copies ran while one was open for 3% of the time, Pallas kernels for 0%

profile of v3, /device:TPU:1, one launch (start us, length us, event | category | flops | bytes accessed | tf_op | source)
XLA Modules:
  0.0 309.0 jit_solution(14502693367635443208)
XLA Ops:
  0.7 0.9 copy.68
  1.5 0.7 fusion.5
  3.0 0.8 fusion.4
  4.7 1.7 scatter_custom_fusion
  6.3 0.7 all_to_all.6
  7.0 7.1 %all-to-all-start = ((s32[32,1,16]{2,1,0:T(1,128)}), s32[32,1,16]{2,1,0:T(1,128)S(1)}, u32[]{:S(2)}, u32[]{:S(2)}) async-start(s32[32,1,16]{2,1,0:T(1,128)} %bitcast.13), calls=%async_computation | async-start | bytes 32768 | tf_op jit(solution)/shard_map/all_to_all | solution.py:741
  14.8 0.8 copy.71
  16.5 1.2 copy.72
  18.2 2.0 pad_maximum_fusion.own_ref
  22.4 0.8 mul.102.weight_col
  23.2 0.8 reshape.278.live_col
  25.5 14.0 %gather_fusion = bf16[512,768]{1,0:T(8,128)(2,1)} fusion(bf16[15664,768]{1,0:T(8,128)(2,1)} %param.23, s32[1024]{0:T(1024)S(1)} %pad_clamp_fusion), kind=kCustom, calls=%fused_computation | custom fusion | bytes 1574912 | tf_op jit(solution)/shard_map/gather | solution.py:745
  39.6 88.6 %shard_map.298 = (bf16[3,32,96,768]{3,2,1,0:T(8,128)(2,1)}, bf16[4,16,128]{2,1,0:T(8,128)(2,1)}, bf16[32,16,768]{2,1,0:T(8,128)(2,1)}) custom-call(bf16[3,8,96,768]{3,2,1,0:T(8,128)(2,1)} %pad_maximum_fusion.own_ref, bf16[16,128]{1,0:T(8,128)(2,1)} %pad.4.bias_ref, bf16[32,16,768]{2,1,0:T(8,128)(2,1)} %bitcast.65), custom_call_target="tpu_custom_call" | custom-call | tf_op jit(solution)/shard_map/pallas_call | solution.py:246
  128.2 0.7 convert_bitcast_fusion
  130.5 39.3 %shard_map.299 = (bf16[256,768]{1,0:T(8,128)(2,1)}, bf16[3,32,96,768]{3,2,1,0:T(8,128)(2,1)}, f32[16,768]{1,0:T(8,128)}, bf16[512,768]{1,0:T(8,128)(2,1)}) custom-call(s32[256,1]{1,0:T(8,128)} %get-tuple-element.44.slot_col, s32[1,256]{1,0:T(1,128)} %add.53.slot_row, f32[256,1]{1,0:T(8,128)} %mul.102.weight_col, f32[256,1]{1,0:T(8,128)} %reshape.278.live_col, ...), custom_call_target="tpu_custom_call" | custom-call | tf_op jit(solution)/shard_map/pallas_call | solution.py:654
  169.7 102.3 %shard_map.300 = (bf16[3,8,96,768]{3,2,1,0:T(8,128)(2,1)}, f32[16,768]{1,0:T(8,128)}, bf16[32,16,768]{2,1,0:T(8,128)(2,1)}) custom-call(bf16[3,32,96,768]{3,2,1,0:T(8,128)(2,1)} %get-tuple-element.29.grad_ref, f32[16,768]{1,0:T(8,128)} %get-tuple-element.30.small_ref, bf16[32,16,768]{2,1,0:T(8,128)(2,1)} %bitcast.72), custom_call_target="tpu_custom_call" | custom-call | tf_op jit(solution)/shard_map/pallas_call | solution.py:422
  272.0 1.2 slice.62
  273.9 0.8 broadcast_multiply_fusion
  275.4 2.6 convert_multiply_fusion
  278.0 0.9 slice_bitcast_fusion.2
  278.8 2.5 slice_bitcast_fusion
  281.6 1.3 convert_multiply_fusion.1
  282.9 1.3 copy.80
  284.5 23.4 %scatter_custom_fusion.1 = f32[15664,768]{1,0:T(8,128)} fusion(s32[512]{0:T(512)S(1)} %reshape.253, f32[512,768]{1,0:T(8,128)S(1)} %bitcast.67, f32[]{:T(128)} %constant.43.clone.1), kind=kCustom, calls=%fused_computation.3 | custom fusion | flops 393216 | bytes 48119812 | tf_op jit(solution)/shard_map/scatter-add | solution.py:796
  (81 shorter events, 10.5 us)
Async XLA Ops:
  0.6 17.3 %copy-start.12 = (s32[4]{0:T(128)S(1)}, s32[4]{0:T(128)}, u32[]{:S(2)}) copy-start(s32[4]{0:T(128)} %param.21) | copy-start | bytes 52
  0.7 17.3 %copy-start.3 = (bf16[192,768]{1,0:T(8,128)(2,1)S(1)}, bf16[192,768]{1,0:T(8,128)(2,1)}, u32[]{:S(2)}) copy-start(bf16[192,768]{1,0:T(8,128)(2,1)} %param.27) | copy-start | bytes 884740
  3.9 14.1 %copy-start = (bf16[768,768]{1,0:T(8,128)(2,1)S(1)}, bf16[768,768]{1,0:T(8,128)(2,1)}, u32[]{:S(2)}) copy-start(bf16[768,768]{1,0:T(8,128)(2,1)} %param.33) | copy-start | bytes 3538948
  4.0 14.1 %copy-start.1 = (bf16[768,768]{1,0:T(8,128)(2,1)S(1)}, bf16[768,768]{1,0:T(8,128)(2,1)}, u32[]{:S(2)}) copy-start(bf16[768,768]{1,0:T(8,128)(2,1)} %param.31) | copy-start | bytes 3538948
  7.0 18.3 %all-to-all-start = ((s32[32,1,16]{2,1,0:T(1,128)}), s32[32,1,16]{2,1,0:T(1,128)S(1)}, u32[]{:S(2)}, u32[]{:S(2)}) async-start(s32[32,1,16]{2,1,0:T(1,128)} %bitcast.13), calls=%async_computation | async-start | bytes 32768 | tf_op jit(solution)/shard_map/all_to_all | solution.py:741
  18.1 3.5 %copy-start.6 = (bf16[768]{0:T(1024)(128)(2,1)S(1)}, bf16[768]{0:T(1024)(128)(2,1)}, u32[]{:S(2)}) copy-start(bf16[768]{0:T(1024)(128)(2,1)} %param.28) | copy-start | bytes 4612
  18.1 3.5 %copy-start.7 = (bf16[768]{0:T(1024)(128)(2,1)S(1)}, bf16[768]{0:T(1024)(128)(2,1)}, u32[]{:S(2)}) copy-start(bf16[768]{0:T(1024)(128)(2,1)} %param.29) | copy-start | bytes 4612
  18.1 3.5 %copy-start.8 = (bf16[768]{0:T(1024)(128)(2,1)S(1)}, bf16[768]{0:T(1024)(128)(2,1)}, u32[]{:S(2)}) copy-start(bf16[768]{0:T(1024)(128)(2,1)} %param.30) | copy-start | bytes 4612
  18.1 3.5 %copy-start.9 = (bf16[768]{0:T(1024)(128)(2,1)S(1)}, bf16[768]{0:T(1024)(128)(2,1)}, u32[]{:S(2)}) copy-start(bf16[768]{0:T(1024)(128)(2,1)} %param.34) | copy-start | bytes 4612
  18.1 3.5 %copy-start.10 = (bf16[768]{0:T(1024)(128)(2,1)S(1)}, bf16[768]{0:T(1024)(128)(2,1)}, u32[]{:S(2)}) copy-start(bf16[768]{0:T(1024)(128)(2,1)} %param.35) | copy-start | bytes 4612
  18.2 3.5 %copy-start.11 = (bf16[768]{0:T(1024)(128)(2,1)S(1)}, bf16[768]{0:T(1024)(128)(2,1)}, u32[]{:S(2)}) copy-start(bf16[768]{0:T(1024)(128)(2,1)} %param.36) | copy-start | bytes 4612
  18.2 5.9 %copy-start.5 = (bf16[768]{0:T(1024)(128)(2,1)S(1)}, bf16[768]{0:T(1024)(128)(2,1)}, u32[]{:S(2)}) copy-start(bf16[768]{0:T(1024)(128)(2,1)} %param.32) | copy-start | bytes 4612
  18.2 5.8 %copy-start.13 = (bf16[192]{0:T(256)(128)(2,1)S(1)}, bf16[192]{0:T(256)(128)(2,1)}, u32[]{:S(2)}) copy-start(bf16[192]{0:T(256)(128)(2,1)} %param.25) | copy-start | bytes 1156
  18.2 5.8 %copy-start.14 = (bf16[192]{0:T(256)(128)(2,1)S(1)}, bf16[192]{0:T(256)(128)(2,1)}, u32[]{:S(2)}) copy-start(bf16[192]{0:T(256)(128)(2,1)} %param.26) | copy-start | bytes 1156
  274.7 3.3 %copy-start.4 = (f32[16,768]{1,0:T(8,128)}, f32[16,768]{1,0:T(8,128)S(1)}, u32[]{:S(2)}) copy-start(f32[16,768]{1,0:T(8,128)S(1)} %broadcast_multiply_fusion) | copy-start | bytes 147460
  282.9 1.4 copy-start.2
  284.5 23.4 %slice-start = ((f32[16,768]{1,0:T(8,128)}), f32[4,768]{1,0:T(4,128)S(1)}, s32[]{:S(2)}) async-start(f32[16,768]{1,0:T(8,128)} %copy-done.4), calls=%async_computation.1 | async-start | bytes 24576 | tf_op jit(solution)/shard_map/slice | solution.py:793
